TPU v7x, 32 devices: a whole 2x2x4 slice. The times are simulated.
32 devices in a mesh: dp: 8 (over y, x, core), tensor: 4 (over z).
Axes of the slice: x: 2, y: 2, z: 4, core: 2. Of those that a mesh axis runs over, the one named last changes fastest.
Arguments:
- block_input: bfloat16 [8, 512, 768], P('dp', 'tensor'), may hold values from -6 to 6
- segment_ids: int32 [8, 512], P('dp', 'tensor'), may hold values from 0 to 3, never falling along the last dimension, each value on 1 to 256 neighbouring positions
- w_qkv: bfloat16 [3, 768, 768], P(None, 'dp', 'tensor'), may hold values from -2.16506351 to 2.16506351
- w_out: bfloat16 [768, 768], P('tensor', 'dp'), may hold values from -0.875 to 0.875
- w_in: bfloat16 [768, 3072], P('dp', 'tensor'), may hold values from -0.21875 to 0.21875
- w_back: bfloat16 [3072, 768], P('tensor', 'dp'), may hold values from -0.21875 to 0.21875
- qv_bias: float32 [2, 768], P(None, 'tensor'), may hold values from -3 to 3
- in_bias: float32 [3072], P('tensor'), may hold values from -3 to 3
- norm_gains: float32 [2, 768], replicated, may hold values from 0.5 to 1.5
- norm_biases: float32 [4, 768], replicated, may hold values from -2 to 2
- out_cotangent: bfloat16 [8, 512, 768], P('dp', 'tensor'), may hold values from -6 to 6
Outputs:
- block_output: bfloat16 [8, 512, 768], P('dp', 'tensor')
- input_grad: float32 [8, 512, 768], P('dp', 'tensor')
- grad_qkv: float32 [3, 768, 768], P(None, 'dp', 'tensor')
- grad_out: float32 [768, 768], P('tensor', 'dp')
- grad_in: float32 [768, 3072], P('dp', 'tensor')
- grad_back: float32 [3072, 768], P('tensor', 'dp')
- grad_qv_bias: float32 [2, 768], P(None, 'tensor')
- grad_in_bias: float32 [3072], P('tensor')
- grad_gains: float32 [2, 768], replicated
- grad_biases: float32 [4, 768], replicated
Inputs may be any that keep to these rules, and one draw needn't show every extreme that they name: `segment_ids`: within each sequence segment numbers never fall; a document spans at most half of 512 tokens, and one document in each sequence spans exactly that many.
All inputs are finite; a program needn't handle non-finite values.
Results may differ from a plain program's by a relative error of at most 0.0098.
Values may be sent and summed in bfloat16 or wider, within the bound.
A program may use at most 64 MiB of HBM per device.

v0:
```python
import math

import jax
import jax.numpy as jnp
from jax import lax
from jax.sharding import PartitionSpec as P

HEAD = 64


EPS = 1e-05
GELU_C = math.sqrt(2.0 / math.pi)
GELU_A = 0.044715


def normalize(residual, gain_row, offset_row):
    centered = residual - jnp.mean(residual, axis=-1, keepdims=True)
    inv_std = lax.rsqrt(jnp.mean(centered * centered, axis=-1, keepdims=True) + EPS)
    normed = centered * inv_std
    return (normed * gain_row + offset_row, normed, inv_std)


def normalize_back(upstream, normed, inv_std, gain_row):
    scaled = upstream * gain_row
    return inv_std * (
        scaled
        - jnp.mean(scaled, axis=-1, keepdims=True)
        - normed * jnp.mean(scaled * normed, axis=-1, keepdims=True)
    )


def gelu_pair(inputs):
    inner_arg = GELU_C * (inputs + GELU_A * inputs * inputs * inputs)
    tangent_h = jnp.tanh(inner_arg)
    value_out = 0.5 * inputs * (1.0 + tangent_h)
    slope_out = 0.5 * (1.0 + tangent_h) + 0.5 * inputs * (1.0 - tangent_h * tangent_h) * GELU_C * (
        1.0 + 3.0 * GELU_A * inputs * inputs
    )
    return (value_out, slope_out)


def contract_rows(left, right):
    return lax.dot_general(
        left, right, (((0,), (0,)), ((), ())), preferred_element_type=jnp.float32
    )


def contract_cols(left, right):
    return lax.dot_general(
        left, right, (((1,), (1,)), ((), ())), preferred_element_type=jnp.float32
    )


def masked_scores(query_block, key_rows, segment, key_end, num_heads):
    block_rows = query_block.shape[0]
    width = query_block.shape[1] // num_heads
    query_heads = query_block.reshape(block_rows, num_heads, width)
    key_heads = key_rows.reshape(key_end, num_heads, width)
    raw_scores = jnp.einsum(
        "qhd,khd->hqk", query_heads, key_heads, preferred_element_type=jnp.float32
    ) * (1.0 / math.sqrt(width))
    query_pos = jnp.arange(block_rows, dtype=jnp.int32)
    key_pos = jnp.arange(key_end, dtype=jnp.int32)
    allowed = (key_pos[None, :] <= query_pos[:, None]) & (segment[None, :] == segment[:, None])
    return jnp.where(allowed[None], raw_scores, -jnp.inf)


def attend_forward(queries, key_rows, values, segment, num_heads):
    total_rows = queries.shape[0]
    block_rows = min(512, total_rows)
    width = queries.shape[1] // num_heads
    scores = masked_scores(queries, key_rows, segment, block_rows, num_heads)
    row_max = jnp.max(scores, axis=-1, keepdims=True)
    log_total = row_max + jnp.log(jnp.sum(jnp.exp(scores - row_max), axis=-1, keepdims=True))
    weights = jnp.exp(scores - log_total).astype(jnp.bfloat16)
    value_heads = values.reshape(block_rows, num_heads, width)
    context = jnp.einsum("hqk,khd->qhd", weights, value_heads, preferred_element_type=jnp.float32)
    contexts = context.reshape(block_rows, num_heads * width).astype(jnp.bfloat16)
    return (contexts, log_total)


def attend_backward(
    queries, key_rows, values, segment, context, log_total, context_grad, num_heads
):
    total_rows = queries.shape[0]
    block_rows = min(512, total_rows)
    width = queries.shape[1] // num_heads
    inv_root = 1.0 / math.sqrt(width)
    key_grad = jnp.zeros((total_rows, num_heads, width), jnp.float32)
    value_grad = jnp.zeros((total_rows, num_heads, width), jnp.float32)
    scores = masked_scores(queries, key_rows, segment, block_rows, num_heads)
    probs = jnp.exp(scores - log_total)
    probs_half = probs.astype(jnp.bfloat16)
    grad_heads = context_grad.reshape(block_rows, num_heads, width)
    context_heads = context.reshape(block_rows, num_heads, width)
    value_heads = values.reshape(block_rows, num_heads, width)
    key_heads = key_rows.reshape(block_rows, num_heads, width)
    query_heads = queries.reshape(block_rows, num_heads, width)
    prob_grad = jnp.einsum(
        "qhd,khd->hqk", grad_heads, value_heads, preferred_element_type=jnp.float32
    )
    row_dot = jnp.transpose(
        jnp.sum(grad_heads.astype(jnp.float32) * context_heads.astype(jnp.float32), axis=-1)
    )[:, :, None]
    score_grad = (probs * (prob_grad - row_dot) * inv_root).astype(jnp.bfloat16)
    query_grads = jnp.einsum(
        "hqk,khd->qhd", score_grad, key_heads, preferred_element_type=jnp.float32
    ).reshape(block_rows, num_heads * width)
    key_grad = key_grad.at[:block_rows].add(
        jnp.einsum("hqk,qhd->khd", score_grad, query_heads, preferred_element_type=jnp.float32)
    )
    value_grad = value_grad.at[:block_rows].add(
        jnp.einsum("hqk,qhd->khd", probs_half, grad_heads, preferred_element_type=jnp.float32)
    )
    return (
        query_grads,
        key_grad.reshape(total_rows, num_heads * width),
        value_grad.reshape(total_rows, num_heads * width),
    )


def shards(
    block_input,
    segment_ids,
    w_qkv,
    w_out,
    w_in,
    w_back,
    qv_bias,
    in_bias,
    norm_gains,
    norm_biases,
    out_cotangent,
):
    residual = block_input[0].astype(jnp.float32)
    local_heads = w_qkv.shape[2] // HEAD
    qkv_full, out_full, in_full, back_full = (
        lax.all_gather(w_qkv, "dp", axis=1, tiled=True),
        lax.all_gather(w_out, "dp", axis=1, tiled=True),
        lax.all_gather(w_in, "dp", axis=0, tiled=True),
        lax.all_gather(w_back, "dp", axis=1, tiled=True),
    )
    first_out, normed_first, inv_first = normalize(residual, norm_gains[0], norm_biases[0])
    first_local = first_out.astype(jnp.bfloat16)
    first_half, segment = (
        lax.all_gather(first_local, "tensor", axis=0, tiled=True),
        lax.all_gather(segment_ids[0], "tensor", axis=0, tiled=True),
    )
    projected = jnp.einsum("sd,cde->sce", first_half, qkv_full, preferred_element_type=jnp.float32)
    queries = (projected[:, 0] + qv_bias[0]).astype(jnp.bfloat16)
    key_rows = projected[:, 1].astype(jnp.bfloat16)
    values = (projected[:, 2] + qv_bias[1]).astype(jnp.bfloat16)
    context, log_total = attend_forward(queries, key_rows, values, segment, local_heads)
    attn_share = lax.psum_scatter(
        jnp.dot(context, out_full, preferred_element_type=jnp.float32),
        "tensor",
        scatter_dimension=0,
        tiled=True,
    )
    middle = residual + attn_share + norm_biases[2]
    second_out, normed_second, inv_second = normalize(middle, norm_gains[1], norm_biases[1])
    second_half = lax.all_gather(second_out.astype(jnp.bfloat16), "tensor", axis=0, tiled=True)
    hidden_pre = jnp.dot(second_half, in_full, preferred_element_type=jnp.float32) + in_bias
    gelu_value, gelu_slope = gelu_pair(hidden_pre)
    activation = gelu_value.astype(jnp.bfloat16)
    mlp_share = lax.psum_scatter(
        jnp.dot(activation, back_full, preferred_element_type=jnp.float32),
        "tensor",
        scatter_dimension=0,
        tiled=True,
    )
    block_out = (middle + mlp_share + norm_biases[3]).astype(jnp.bfloat16)
    qkv_back_w, out_back_w, in_back_w, back_back_w = (
        lax.all_gather(w_qkv, "dp", axis=1, tiled=True),
        lax.all_gather(w_out, "dp", axis=1, tiled=True),
        lax.all_gather(w_in, "dp", axis=0, tiled=True),
        lax.all_gather(w_back, "dp", axis=1, tiled=True),
    )
    cotangent = out_cotangent[0].astype(jnp.float32)
    cotangent_full = lax.all_gather(out_cotangent[0], "tensor", axis=0, tiled=True)
    grad_back_part = contract_rows(activation, cotangent_full)
    hidden_grad = contract_cols(cotangent_full, back_back_w) * gelu_slope
    hidden_half = hidden_grad.astype(jnp.bfloat16)
    grad_in_part = contract_rows(second_half, hidden_half)
    second_grad = lax.psum_scatter(
        contract_cols(hidden_half, in_back_w), "tensor", scatter_dimension=0, tiled=True
    )
    middle_grad = cotangent + normalize_back(second_grad, normed_second, inv_second, norm_gains[1])
    middle_full = lax.all_gather(middle_grad.astype(jnp.bfloat16), "tensor", axis=0, tiled=True)
    grad_out_part = contract_rows(context, middle_full)
    context_grad = contract_cols(middle_full, out_back_w).astype(jnp.bfloat16)
    query_grad, key_grad, value_grad = attend_backward(
        queries, key_rows, values, segment, context, log_total, context_grad, local_heads
    )
    proj_half = jnp.stack([query_grad, key_grad, value_grad], axis=1).astype(jnp.bfloat16)
    grad_qkv_part = jnp.einsum(
        "sd,sce->cde", first_half, proj_half, preferred_element_type=jnp.float32
    )
    first_grad = lax.psum_scatter(
        jnp.einsum("sce,cde->sd", proj_half, qkv_back_w, preferred_element_type=jnp.float32),
        "tensor",
        scatter_dimension=0,
        tiled=True,
    )
    input_grad = middle_grad + normalize_back(first_grad, normed_first, inv_first, norm_gains[0])
    grad_qkv, grad_out, grad_in, grad_back = (
        lax.psum_scatter(grad_qkv_part, "dp", scatter_dimension=1, tiled=True),
        lax.psum_scatter(grad_out_part, "dp", scatter_dimension=1, tiled=True),
        lax.psum_scatter(grad_in_part, "dp", scatter_dimension=0, tiled=True),
        lax.psum_scatter(grad_back_part, "dp", scatter_dimension=1, tiled=True),
    )
    head_terms = jnp.stack([jnp.sum(query_grad, axis=0), jnp.sum(value_grad, axis=0)])
    grad_qv_bias, grad_in_bias = lax.psum((head_terms, jnp.sum(hidden_grad, axis=0)), "dp")
    gain_terms = jnp.stack(
        [jnp.sum(first_grad * normed_first, axis=0), jnp.sum(second_grad * normed_second, axis=0)]
    )
    offset_terms = jnp.stack(
        [
            jnp.sum(first_grad, axis=0),
            jnp.sum(second_grad, axis=0),
            jnp.sum(middle_grad, axis=0),
            jnp.sum(cotangent, axis=0),
        ]
    )
    grad_gains, grad_biases = lax.psum((gain_terms, offset_terms), ("dp", "tensor"))
    return (
        block_out[None],
        input_grad[None],
        grad_qkv,
        grad_out,
        grad_in,
        grad_back,
        grad_qv_bias,
        grad_in_bias,
        grad_gains,
        grad_biases,
    )


def solution(mesh):
    in_specs = (
        P("dp", "tensor", None),
        P("dp", "tensor"),
        P(None, "dp", "tensor"),
        P("tensor", "dp"),
        P("dp", "tensor"),
        P("tensor", "dp"),
        P(None, "tensor"),
        P("tensor"),
        P(),
        P(),
        P("dp", "tensor", None),
    )
    out_specs = (
        P("dp", "tensor", None),
        P("dp", "tensor", None),
        P(None, "dp", "tensor"),
        P("tensor", "dp"),
        P("dp", "tensor"),
        P("tensor", "dp"),
        P(None, "tensor"),
        P("tensor"),
        P(),
        P(),
    )
    return jax.shard_map(shards, mesh=mesh, in_specs=in_specs, out_specs=out_specs, check_vma=False)
```

profile of v0, /device:TPU:0, one launch (start us, length us, event | category | flops | bytes accessed | tf_op | source)
XLA Modules:
  0.0 469.2 jit_solution(12906367978198578888)
XLA Ops:
  8.1 1.1 convert_reduce_fusion.1
  9.2 1.1 fusion.29
  10.3 1.5 slice_reduce_fusion
  11.8 0.8 slice_reduce_fusion.2
  12.6 1.1 fusion.22
  13.7 21.3 %all_gather.31 = bf16[512,768]{1,0:T(8,128)(2,1)S(1)} all-gather(bf16[128,768]{1,0:T(8,128)(2,1)S(1)} %fusion.22), channel_id=1, replica_groups=mesh['dp'=8,'tensor'=4] {'tensor'}, dimensions={0}, use_global_device_ids=true | all-gather | bytes 983040 | tf_op jit(solution)/shard_map/all_gather | solution.py:146
  35.2 13.2 %all_gather.32 = bf16[3,768,192]{2,0,1:T(4,128)(2,1)S(1)} all-gather(bf16[3,96,192]{2,0,1:T(4,128)(2,1)S(1)} %copy.29), channel_id=1, replica_groups=mesh['dp'=8,'tensor'=4] {'dp'}, dimensions={1}, use_global_device_ids=true | all-gather | bytes 995328 | tf_op jit(solution)/shard_map/all_gather | solution.py:138
  48.3 0.9 copy.30
  49.9 0.8 fusion.47
  50.7 0.8 slice.97
  51.5 9.2 %all-gather = s32[1,512]{1,0:T(1,128)S(1)} all-gather(s32[1,128]{1,0:T(1,128)S(1)} %copy-done.46), channel_id=2, replica_groups=mesh['dp'=8,'tensor'=4] {'tensor'}, dimensions={1}, use_global_device_ids=true | all-gather | bytes 2560 | tf_op jit(solution)/shard_map/all_gather | solution.py:147
  60.7 0.9 fusion.8
  62.3 1.9 fusion.1
  64.2 0.7 exponential_reduce_fusion
  65.2 8.4 %all_gather.34 = bf16[192,768]{0,1:T(8,128)(2,1)S(1)} all-gather(bf16[192,96]{0,1:T(8,128)(2,1)S(1)} %copy.32), channel_id=1, replica_groups=mesh['dp'=8,'tensor'=4] {'dp'}, dimensions={1}, use_global_device_ids=true | all-gather | bytes 331776 | tf_op jit(solution)/shard_map/all_gather | solution.py:139
  73.6 2.1 convolution_convert_fusion.2
  75.7 0.7 copy-done.16
  76.4 1.6 fusion.52
  79.2 29.8 %all-gather.1 = bf16[1,512,768]{2,1,0:T(8,128)(2,1)} all-gather(bf16[1,128,768]{2,1,0:T(8,128)(2,1)S(1)} %copy-done.18), channel_id=3, replica_groups=mesh['dp'=8,'tensor'=4] {'tensor'}, dimensions={1}, use_global_device_ids=true | all-gather | bytes 983040 | tf_op jit(solution)/shard_map/all_gather | solution.py:180
  109.1 13.7 %reduce-scatter.13.cloned.1.call-done = f32[128,768]{1,0:T(8,128)} async-done(((f32[512,768]{1,0:T(8,128)}), f32[128,768]{1,0:T(8,128)}) %reduce-scatter.13.cloned.1.call-update) | async-done | bytes 393232 | tf_op jit(solution)/shard_map/reduce_scatter | solution.py:154
  122.7 1.2 fusion.45
  124.5 0.8 add_convert_fusion.1
  125.4 18.4 %all_gather.35 = bf16[512,768]{1,0:T(8,128)(2,1)} all-gather(bf16[128,768]{1,0:T(8,128)(2,1)S(1)} %add_convert_fusion.1), channel_id=1, replica_groups=mesh['dp'=8,'tensor'=4] {'tensor'}, dimensions={0}, use_global_device_ids=true | all-gather | bytes 983040 | tf_op jit(solution)/shard_map/all_gather | solution.py:162
  143.7 3.4 convolution_add_fusion
  147.2 4.1 fusion.50
  151.3 0.9 copy-done.22
  152.2 2.0 fusion.34
  154.2 4.0 fusion.42
  158.3 30.3 %reduce-scatter.17.cloned.1.call-done = f32[128,768]{1,0:T(8,128)} async-done(((f32[512,768]{1,0:T(8,128)}), f32[128,768]{1,0:T(8,128)}) %reduce-scatter.17.cloned.1.call-update) | async-done | bytes 393232 | tf_op jit(solution)/shard_map/reduce_scatter | solution.py:185
  188.6 1.8 multiply_reduce_fusion
  190.9 34.3 %reduce-scatter.15.cloned.1.call-done = f32[128,768]{1,0:T(8,128)} async-done(((f32[512,768]{1,0:T(8,128)}), f32[128,768]{1,0:T(8,128)}) %reduce-scatter.15.cloned.1.call-update) | async-done | bytes 393232 | tf_op jit(solution)/shard_map/reduce_scatter | solution.py:166
  225.2 2.7 fusion.43
  228.0 0.7 copy-done.7
  228.7 18.1 %all_gather.39 = bf16[512,768]{1,0:T(8,128)(2,1)S(1)} all-gather(bf16[128,768]{1,0:T(8,128)(2,1)S(1)} %convert_element_type.84), channel_id=1, replica_groups=mesh['dp'=8,'tensor'=4] {'tensor'}, dimensions={0}, use_global_device_ids=true | all-gather | bytes 983040 | tf_op jit(solution)/shard_map/all_gather | solution.py:189
  246.8 1.1 convolution_convert_fusion.1
  248.0 1.3 convolution_bitcast_fusion.2
  249.3 1.1 multiply_reduce_fusion.1
  250.4 2.5 multiply_convert_fusion
  252.9 1.1 copy-done.1
  254.1 1.3 convolution_convert_fusion
  255.4 2.0 fusion.48
  257.5 1.0 fusion.49
  258.5 0.7 copy-done.48
  259.2 1.8 convolution_bitcast_fusion
  261.1 3.0 copy.44
  264.1 2.8 reshape.220
  267.0 1.1 copy-done.4
  268.2 2.0 convolution_bitcast_fusion.1
  270.2 1.1 copy-done.2
  271.5 2.2 fusion.32
  273.8 1.1 copy-done.20
  275.5 2.4 fusion.10
  278.0 0.8 copy-done.19
  279.2 12.7 %all-reduce.1 = (f32[2,192]{1,0:T(2,128)}, f32[768]{0:T(1024)}) all-reduce(f32[2,192]{1,0:T(2,128)S(1)} %pad_maximum_fusion.5, f32[768]{0:T(1024)S(1)} %copy-done.41), channel_id=1, replica_groups=mesh['dp'=8,'tensor'=4] {'dp'}, use_global_device_ids=true, to_apply=%region_21.22 | all-reduce | flops 1152 | bytes 9216 | tf_op jit(solution)/shard_map/psum | solution.py:213
  291.8 1.6 copy.47
  293.5 39.7 %reduce-scatter.25.cloned.1.call-done = f32[96,576]{1,0:T(8,128)} async-done(((f32[768,576]{1,0:T(8,128)}), f32[96,576]{1,0:T(8,128)}) %reduce-scatter.25.cloned.1.call-update) | async-done | bytes 221200
  333.2 1.1 reshape.221
  334.3 0.8 copy.38
  335.1 35.9 %reduce-scatter.19.cloned.1.call-done = f32[128,768]{1,0:T(8,128)} async-done(((f32[512,768]{1,0:T(8,128)}), f32[128,768]{1,0:T(8,128)}) %reduce-scatter.19.cloned.1.call-update) | async-done | bytes 393232 | tf_op jit(solution)/shard_map/reduce_scatter | solution.py:199
  371.0 1.2 fusion.28
  372.3 39.5 %all-reduce = (f32[2,768]{1,0:T(2,128)}, f32[4,768]{1,0:T(4,128)}) all-reduce(f32[2,768]{1,0:T(2,128)S(1)} %pad_maximum_fusion.4, f32[4,768]{1,0:T(4,128)S(1)} %pad_maximum_fusion.3), channel_id=1, replica_groups=mesh['dp'=8,'tensor'=4] {'dp','tensor'}, use_global_device_ids=true, to_apply=%region_26.27 | all-reduce | flops 4608 | bytes 36864 | tf_op jit(solution)/shard_map/psum | solution.py:225
  411.8 1.9 fusion.27
  413.7 2.3 reduce-scatter.21.cloned.1.call-done
  416.0 46.0 %reduce-scatter.23.cloned.1.call-done = f32[768,96]{0,1:T(8,128)} async-done(((f32[768,768]{0,1:T(8,128)}), f32[768,96]{0,1:T(8,128)}) %reduce-scatter.23.cloned.1.call-update) | async-done | bytes 294928 | tf_op jit(solution)/shard_map/reduce_scatter | solution.py:210
  (144 shorter events, 5.8 us)
Async XLA Ops:
  8.0 27.0 %copy-start.28 = (bf16[3,96,192]{2,1,0:T(8,128)(2,1)S(1)}, bf16[3,96,192]{2,1,0:T(8,128)(2,1)}, u32[]{:S(2)}) copy-start(bf16[3,96,192]{2,1,0:T(8,128)(2,1)} %param.21) | copy-start | bytes 331780
  8.0 114.7 %reduce-scatter.13.cloned.1.call-start = ((), (), s32[]{:S(2)}) async-start(), calls=%async_computation.8 | async-start | bytes 1966080 | tf_op jit(solution)/shard_map/reduce_scatter | solution.py:154
  9.1 26.0 %copy-start.33 = (f32[128]{0:T(128)}, f32[128]{0:T(128)S(1)}, u32[]{:S(2)}) copy-start(f32[128]{0:T(128)S(1)} %broadcast_multiply_fusion.5) | copy-start | bytes 1540
  10.3 24.9 %copy-start.38 = (f32[128]{0:T(128)}, f32[128]{0:T(128)S(1)}, u32[]{:S(2)}) copy-start(f32[128]{0:T(128)S(1)} %add_rsqrt_fusion.1) | copy-start | bytes 1540
  35.0 14.2 %copy-start.11 = (bf16[512,768]{1,0:T(8,128)(2,1)}, bf16[512,768]{1,0:T(8,128)(2,1)S(1)}, u32[]{:S(2)}) copy-start(bf16[512,768]{1,0:T(8,128)(2,1)S(1)} %all_gather.31) | copy-start | bytes 2359300
  49.2 1.5 copy-start.3
  49.9 1.6 copy-start.46
  49.9 11.7 %copy-start.45 = (f32[2,192]{1,0:T(2,128)S(1)}, f32[2,192]{1,0:T(2,128)}, u32[]{:S(2)}) copy-start(f32[2,192]{1,0:T(2,128)} %param.25) | copy-start | bytes 4612
  50.7 13.5 %copy-start.5 = (f32[512,1,192]{0,2,1:T(8,128)}, f32[512,1,192]{0,2,1:T(8,128)S(1)}, u32[]{:S(2)}) copy-start(f32[512,1,192]{0,2,1:T(8,128)S(1)} %get-tuple-element.94) | copy-start | bytes 1179652
  62.3 1.9 copy-start.13
  64.2 0.8 copy-start.42
  64.2 0.9 copy-start.29
  64.2 9.4 %copy-start.14 = (pred[512,512]{0,1:T(8,128)(4,1)S(1)}, pred[512,512]{0,1:T(8,128)(4,1)}, u32[]{:S(2)}) copy-start(pred[512,512]{0,1:T(8,128)(4,1)} %fusion.8) | copy-start | bytes 786436
  64.9 10.8 %copy-start.36 = (f32[3,512]{1,0:T(4,128)}, f32[3,512]{1,0:T(4,128)S(1)}, u32[]{:S(2)}) copy-start(f32[3,512]{1,0:T(4,128)S(1)} %log_add_fusion) | copy-start | bytes 18436
  65.0 10.7 %copy-start.43 = (f32[3,64]{1,0:T(4,128)}, f32[3,64]{1,0:T(4,128)S(1)}, u32[]{:S(2)}) copy-start(f32[3,64]{1,0:T(4,128)S(1)} %add.161) | copy-start | bytes 2308
  73.6 2.1 copy-start.9
  75.7 0.7 copy-start.16
  76.4 2.8 copy-start.18
  78.0 65.7 %all-gather.5.cloned.1.call-start = ((), (), s32[]{:S(2)}) async-start(), calls=%async_computation.9 | async-start | bytes 1327104 | tf_op jit(solution)/shard_map/all_gather | solution.py:140
  78.6 68.6 %all-gather.7.cloned.1.call-start = ((), (), s32[]{:S(2)}) async-start(), calls=%async_computation.10 | async-start | bytes 1327104 | tf_op jit(solution)/shard_map/all_gather | solution.py:141
  79.2 109.4 %reduce-scatter.17.cloned.1.call-start = ((), (), s32[]{:S(2)}) async-start(), calls=%async_computation.12 | async-start | bytes 1966080 | tf_op jit(solution)/shard_map/reduce_scatter | solution.py:185
  123.9 0.6 copy-start.35
  124.2 1.2 copy-start.40
  147.2 5.0 %copy-start.47 = (bf16[768,768]{1,0:T(8,128)(2,1)S(1)}, bf16[768,768]{1,0:T(8,128)(2,1)}, u32[]{:S(2)}) copy-start(bf16[768,768]{1,0:T(8,128)(2,1)} %all-gather.5.cloned.1.call-done) | copy-start | bytes 3538948
  151.3 0.9 copy-start.22
  154.2 71.0 %reduce-scatter.15.cloned.1.call-start = ((), (), s32[]{:S(2)}) async-start(), calls=%async_computation.11 | async-start | bytes 1966080 | tf_op jit(solution)/shard_map/reduce_scatter | solution.py:166
  158.2 133.6 %reduce-scatter.27.cloned.1.call-start = ((), (), s32[]{:S(2)}) async-start(), calls=%async_computation.17 | async-start | bytes 884736
  225.2 21.6 %copy-start.10 = (bf16[192,768]{0,1:T(8,128)(2,1)S(1)}, bf16[192,768]{0,1:T(8,128)(2,1)}, u32[]{:S(2)}) copy-start(bf16[192,768]{0,1:T(8,128)(2,1)} %copy-done.9) | copy-start | bytes 884740
  228.0 0.7 copy-start.7
  228.0 20.0 %copy-start.17 = (bf16[3,64,512]{2,1,0:T(8,128)(2,1)S(1)}, bf16[3,64,512]{2,1,0:T(8,128)(2,1)}, u32[]{:S(2)}) copy-start(bf16[3,64,512]{2,1,0:T(8,128)(2,1)} %copy-done.16) | copy-start | bytes 589828
  246.8 3.6 copy-start.15
  246.8 3.6 copy-start.37
  246.8 3.6 copy-start.44
  250.4 3.6 copy-start.6
  252.9 1.2 copy-start.1
  255.4 77.8 %reduce-scatter.25.cloned.1.call-start = ((), (), s32[]{:S(2)}) async-start(), calls=%async_computation.16 | async-start | bytes 2211840
  255.4 2.0 copy-start.21
  257.5 1.1 copy-start.26
  257.5 1.8 copy-start.12
  257.5 1.7 copy-start.24
  258.5 0.7 copy-start.48
  266.9 1.2 copy-start.4
  266.9 1.2 copy-start.25
  266.9 1.2 copy-start.27
  266.9 1.3 copy-start.49
  266.9 104.0 %reduce-scatter.19.cloned.1.call-start = ((), (), s32[]{:S(2)}) async-start(), calls=%async_computation.13 | async-start | bytes 1966080 | tf_op jit(solution)/shard_map/reduce_scatter | solution.py:199
  270.2 1.1 copy-start.2
  270.2 1.4 copy-start.23
  270.2 145.8 %reduce-scatter.21.cloned.1.call-start = ((), (), s32[]{:S(2)}) async-start(), calls=%async_computation.14 | async-start | bytes 2654208 | tf_op jit(solution)/shard_map/reduce_scatter | solution.py:209
  273.8 1.2 copy-start.20
  273.8 1.8 copy-start.50
  273.8 188.3 %reduce-scatter.23.cloned.1.call-start = ((), (), s32[]{:S(2)}) async-start(), calls=%async_computation.15 | async-start | bytes 2654208 | tf_op jit(solution)/shard_map/reduce_scatter | solution.py:210
  277.9 0.9 copy-start.19
  277.9 1.0 copy-start.32
  277.9 1.0 copy-start.31
  277.9 1.0 copy-start.30
  277.9 1.2 copy-start.41
  278.0 93.0 %copy-start = (bf16[1,128,768]{2,1,0:T(8,128)(2,1)S(1)}, bf16[1,128,768]{2,1,0:T(8,128)(2,1)}, u32[]{:S(2)}) copy-start(bf16[1,128,768]{2,1,0:T(8,128)(2,1)} %param.19) | copy-start | bytes 589828
  278.0 93.0 %copy-start.34 = (f32[128]{0:T(128)S(1)}, f32[128]{0:T(128)}, u32[]{:S(2)}) copy-start(f32[128]{0:T(128)} %copy-done.33) | copy-start | bytes 1540
  278.0 93.0 %copy-start.39 = (f32[128]{0:T(128)S(1)}, f32[128]{0:T(128)}, u32[]{:S(2)}) copy-start(f32[128]{0:T(128)} %copy-done.38) | copy-start | bytes 1540
  278.9 132.9 %copy-start.8 = (f32[128,768]{1,0:T(8,128)S(1)}, f32[128,768]{1,0:T(8,128)}, u32[]{:S(2)}) copy-start(f32[128,768]{1,0:T(8,128)} %copy-done.7) | copy-start | bytes 1179652
Sparse Core Ops, SparseCore 0:
  78.1 44.5 reduce-scatter.12
  154.3 34.2 reduce-scatter.16
  190.9 34.2 reduce-scatter.14
Sparse Core Ops, SparseCore 1:
  80.4 21.2 all-gather.4
  103.4 23.8 all-gather.6
  255.4 34.1 reduce-scatter.26
  293.0 40.1 reduce-scatter.24
  335.5 35.4 reduce-scatter.18
  374.9 41.1 reduce-scatter.20
  419.8 42.2 reduce-scatter.22
where the time goes:
time: 470 us; the launch traced here: 469 us
  waiting for transfers between devices  203 us (43%)
  blocking collectives  171 us (36%)
  matrix products  37.4 us (8%)
  local copies, waits for them, and re-layouts  24.9 us (5%)
  other arithmetic  16.6 us (4%)
  between operations  15.9 us (3%)
    reduce_scatter x1, waiting for transfers between devices, shards(): lax.psum_scatter(grad_back_part, 'dp', scatter_dimension=1, tiled=True)  46 us
    unnamed x12, waiting for transfers between devices  40.9 us
    psum x1, blocking collectives, shards(): lax.psum((gain_terms, offset_terms), ('dp', 'tensor'))  39.5 us
    reduce_scatter x1, waiting for transfers between devices, shards(): lax.psum_scatter(jnp.einsum('sce,cde->sd', proj_half, qkv_back_w, preferr...  35.9 us
    reduce_scatter x1, waiting for transfers between devices, shards(): lax.psum_scatter(jnp.dot(activation, back_full, preferred_element_type=jn...  34.3 us
    reduce_scatter x1, waiting for transfers between devices, shards(): lax.psum_scatter(contract_cols(hidden_half, in_back_w), 'tensor', scatter...  30.3 us
    all_gather x1, blocking collectives, shards(): lax.all_gather(out_cotangent[0], 'tensor', axis=0, tiled=True)  29.8 us
    all_gather x1, blocking collectives, shards(): lax.all_gather(first_local, 'tensor', axis=0, tiled=True)  21.3 us
  transfers between devices with their start and end apart: 10, of which 7 were waited for; matrix products, arithmetic and copies ran while one was open for 8% of the time, Pallas kernels for 0%

commit v1 on v0

--- a/solution.py
+++ b/solution.py
@@ -119,6 +119,12 @@
     )
 
 
+def half_scatter(share):
+    return lax.psum_scatter(
+        share.astype(jnp.bfloat16), "tensor", scatter_dimension=0, tiled=True
+    ).astype(jnp.float32)
+
+
 def shards(
     block_input,
     segment_ids,
@@ -132,97 +138,85 @@
     norm_biases,
     out_cotangent,
 ):
+    bf16 = jnp.bfloat16
     residual = block_input[0].astype(jnp.float32)
-    local_heads = w_qkv.shape[2] // HEAD
-    qkv_full, out_full, in_full, back_full = (
-        lax.all_gather(w_qkv, "dp", axis=1, tiled=True),
-        lax.all_gather(w_out, "dp", axis=1, tiled=True),
-        lax.all_gather(w_in, "dp", axis=0, tiled=True),
-        lax.all_gather(w_back, "dp", axis=1, tiled=True),
-    )
+    head_cols = w_qkv.shape[2]
+    hidden_cols = w_in.shape[1]
+    local_heads = head_cols // HEAD
+    cuts = [head_cols, 2 * head_cols, 3 * head_cols, 4 * head_cols, 4 * head_cols + hidden_cols]
+    packed = jnp.concatenate([w_qkv[0], w_qkv[1], w_qkv[2], w_out.T, w_in, w_back.T], axis=1)
+    full = lax.all_gather(packed, "dp", axis=0, tiled=True)
+    qkv_full = full[:, : cuts[2]]
+    out_full = full[:, cuts[2] : cuts[3]]
+    in_full = full[:, cuts[3] : cuts[4]]
+    back_full = full[:, cuts[4] :]
     first_out, normed_first, inv_first = normalize(residual, norm_gains[0], norm_biases[0])
-    first_local = first_out.astype(jnp.bfloat16)
-    first_half, segment = (
-        lax.all_gather(first_local, "tensor", axis=0, tiled=True),
+    first_half, segment, cotangent_full = (
+        lax.all_gather(first_out.astype(bf16), "tensor", axis=0, tiled=True),
         lax.all_gather(segment_ids[0], "tensor", axis=0, tiled=True),
-    )
-    projected = jnp.einsum("sd,cde->sce", first_half, qkv_full, preferred_element_type=jnp.float32)
-    queries = (projected[:, 0] + qv_bias[0]).astype(jnp.bfloat16)
-    key_rows = projected[:, 1].astype(jnp.bfloat16)
-    values = (projected[:, 2] + qv_bias[1]).astype(jnp.bfloat16)
+        lax.all_gather(out_cotangent[0], "tensor", axis=0, tiled=True),
+    )
+    projected = jnp.dot(first_half, qkv_full, preferred_element_type=jnp.float32)
+    queries = (projected[:, : cuts[0]] + qv_bias[0]).astype(bf16)
+    key_rows = projected[:, cuts[0] : cuts[1]].astype(bf16)
+    values = (projected[:, cuts[1] :] + qv_bias[1]).astype(bf16)
     context, log_total = attend_forward(queries, key_rows, values, segment, local_heads)
-    attn_share = lax.psum_scatter(
-        jnp.dot(context, out_full, preferred_element_type=jnp.float32),
-        "tensor",
-        scatter_dimension=0,
-        tiled=True,
-    )
+    attn_share = half_scatter(contract_cols(context, out_full))
     middle = residual + attn_share + norm_biases[2]
     second_out, normed_second, inv_second = normalize(middle, norm_gains[1], norm_biases[1])
-    second_half = lax.all_gather(second_out.astype(jnp.bfloat16), "tensor", axis=0, tiled=True)
+    second_half = lax.all_gather(second_out.astype(bf16), "tensor", axis=0, tiled=True)
     hidden_pre = jnp.dot(second_half, in_full, preferred_element_type=jnp.float32) + in_bias
     gelu_value, gelu_slope = gelu_pair(hidden_pre)
-    activation = gelu_value.astype(jnp.bfloat16)
-    mlp_share = lax.psum_scatter(
-        jnp.dot(activation, back_full, preferred_element_type=jnp.float32),
-        "tensor",
-        scatter_dimension=0,
-        tiled=True,
-    )
-    block_out = (middle + mlp_share + norm_biases[3]).astype(jnp.bfloat16)
-    qkv_back_w, out_back_w, in_back_w, back_back_w = (
-        lax.all_gather(w_qkv, "dp", axis=1, tiled=True),
-        lax.all_gather(w_out, "dp", axis=1, tiled=True),
-        lax.all_gather(w_in, "dp", axis=0, tiled=True),
-        lax.all_gather(w_back, "dp", axis=1, tiled=True),
-    )
+    activation = gelu_value.astype(bf16)
+    mlp_share = half_scatter(contract_cols(activation, back_full))
+    block_out = (middle + mlp_share + norm_biases[3]).astype(bf16)
     cotangent = out_cotangent[0].astype(jnp.float32)
-    cotangent_full = lax.all_gather(out_cotangent[0], "tensor", axis=0, tiled=True)
-    grad_back_part = contract_rows(activation, cotangent_full)
-    hidden_grad = contract_cols(cotangent_full, back_back_w) * gelu_slope
-    hidden_half = hidden_grad.astype(jnp.bfloat16)
+    grad_back_part = contract_rows(cotangent_full, activation)
+    hidden_grad = jnp.dot(cotangent_full, back_full, preferred_element_type=jnp.float32) * gelu_slope
+    hidden_half = hidden_grad.astype(bf16)
     grad_in_part = contract_rows(second_half, hidden_half)
-    second_grad = lax.psum_scatter(
-        contract_cols(hidden_half, in_back_w), "tensor", scatter_dimension=0, tiled=True
-    )
+    second_grad = half_scatter(contract_cols(hidden_half, in_full))
     middle_grad = cotangent + normalize_back(second_grad, normed_second, inv_second, norm_gains[1])
-    middle_full = lax.all_gather(middle_grad.astype(jnp.bfloat16), "tensor", axis=0, tiled=True)
-    grad_out_part = contract_rows(context, middle_full)
-    context_grad = contract_cols(middle_full, out_back_w).astype(jnp.bfloat16)
+    middle_full = lax.all_gather(middle_grad.astype(bf16), "tensor", axis=0, tiled=True)
+    grad_out_part = contract_rows(middle_full, context)
+    context_grad = jnp.dot(middle_full, out_full, preferred_element_type=jnp.float32).astype(bf16)
     query_grad, key_grad, value_grad = attend_backward(
         queries, key_rows, values, segment, context, log_total, context_grad, local_heads
     )
-    proj_half = jnp.stack([query_grad, key_grad, value_grad], axis=1).astype(jnp.bfloat16)
-    grad_qkv_part = jnp.einsum(
-        "sd,sce->cde", first_half, proj_half, preferred_element_type=jnp.float32
-    )
-    first_grad = lax.psum_scatter(
-        jnp.einsum("sce,cde->sd", proj_half, qkv_back_w, preferred_element_type=jnp.float32),
-        "tensor",
-        scatter_dimension=0,
-        tiled=True,
-    )
+    proj_half = jnp.concatenate([query_grad, key_grad, value_grad], axis=1).astype(bf16)
+    grad_qkv_part = contract_rows(first_half, proj_half)
+    first_grad = half_scatter(contract_cols(proj_half, qkv_full))
     input_grad = middle_grad + normalize_back(first_grad, normed_first, inv_first, norm_gains[0])
-    grad_qkv, grad_out, grad_in, grad_back = (
-        lax.psum_scatter(grad_qkv_part, "dp", scatter_dimension=1, tiled=True),
-        lax.psum_scatter(grad_out_part, "dp", scatter_dimension=1, tiled=True),
-        lax.psum_scatter(grad_in_part, "dp", scatter_dimension=0, tiled=True),
-        lax.psum_scatter(grad_back_part, "dp", scatter_dimension=1, tiled=True),
-    )
-    head_terms = jnp.stack([jnp.sum(query_grad, axis=0), jnp.sum(value_grad, axis=0)])
-    grad_qv_bias, grad_in_bias = lax.psum((head_terms, jnp.sum(hidden_grad, axis=0)), "dp")
-    gain_terms = jnp.stack(
-        [jnp.sum(first_grad * normed_first, axis=0), jnp.sum(second_grad * normed_second, axis=0)]
-    )
-    offset_terms = jnp.stack(
+    parts = jnp.concatenate(
+        [grad_qkv_part, grad_out_part, grad_in_part, grad_back_part], axis=1
+    ).astype(bf16)
+    grads = lax.psum_scatter(parts, "dp", scatter_dimension=0, tiled=True).astype(jnp.float32)
+    grad_qkv = jnp.stack([grads[:, : cuts[0]], grads[:, cuts[0] : cuts[1]], grads[:, cuts[1] : cuts[2]]])
+    grad_out = grads[:, cuts[2] : cuts[3]].T
+    grad_in = grads[:, cuts[3] : cuts[4]]
+    grad_back = grads[:, cuts[4] :].T
+    own = jnp.concatenate(
+        [jnp.sum(query_grad, axis=0), jnp.sum(value_grad, axis=0), jnp.sum(hidden_grad, axis=0)]
+    )
+    tensors = lax.axis_size("tensor")
+    rank = lax.axis_index("tensor")
+    spread = jnp.where(jnp.arange(tensors)[:, None] == rank, own[None], 0.0)
+    norm_terms = jnp.stack(
         [
+            jnp.sum(first_grad * normed_first, axis=0),
+            jnp.sum(second_grad * normed_second, axis=0),
             jnp.sum(first_grad, axis=0),
             jnp.sum(second_grad, axis=0),
             jnp.sum(middle_grad, axis=0),
             jnp.sum(cotangent, axis=0),
         ]
     )
-    grad_gains, grad_biases = lax.psum((gain_terms, offset_terms), ("dp", "tensor"))
+    total = lax.psum(
+        jnp.concatenate([spread.reshape(-1), norm_terms.reshape(-1)]), ("dp", "tensor")
+    )
+    width = own.shape[0]
+    own_total = lax.dynamic_slice(total, (rank * width,), (width,))
+    norm_total = total[tensors * width :].reshape(norm_terms.shape)
     return (
         block_out[None],
         input_grad[None],
@@ -230,10 +224,10 @@
         grad_out,
         grad_in,
         grad_back,
-        grad_qv_bias,
-        grad_in_bias,
-        grad_gains,
-        grad_biases,
+        own_total[: 2 * head_cols].reshape(2, head_cols),
+        own_total[2 * head_cols :],
+        norm_total[:2],
+        norm_total[2:],
     )
 
 

time: 470 us -> 283 us (0.60)
  waiting for transfers between devices: 203 us -> 63.7 us
  blocking collectives: 171 us -> 135 us
  matrix products: 37.4 us -> 27.2 us
    reduce_scatter x6 -> x4, waiting for transfers between devices: 162 us -> 52.2 us  [half_scatter(): lax.psum_scatter(share.astype(jnp.bfloat16), 'tensor', scatter_dimension=...]
    unnamed x12 -> x7, waiting for transfers between devices: 40.9 us -> 6.17 us
    all_gather x5 -> x3, blocking collectives: 79.4 us -> 54.3 us  [the longest x1 19.5 us: shards(): lax.all_gather(second_out.astype(bf16), 'tensor', axis=0, tiled=True)]
    psum x2 -> x1, blocking collectives: 52.2 us -> 39.2 us  [shards(): lax.psum(jnp.concatenate([spread.reshape(-1), norm_terms.reshape(-1)]), (...]
    all_gather x2 -> x1, waiting for transfers between devices: 0.01 us -> 5.32 us  [shards(): full = lax.all_gather(packed, 'dp', axis=0, tiled=True)]
    dot_general x3 -> x4, matrix products: 7.2 us -> 11.1 us  [contract_cols(): lax.dot_general(left, right, (((1,), (1,)), ((), ())), preferred_element_...]
    unnamed x109 -> x102, local copies, waits for them, and re-layouts: 19.2 us -> 18 us
  transfers between devices with their start and end apart: 10 -> 6, of which waited for: 7 -> 6; matrix products, arithmetic and copies ran while one was open for 8% -> 9% of each run, Pallas kernels for 0% -> 0%
where the time goes in v1:
time: 283 us; the launch traced here: 282 us
  blocking collectives  135 us (48%)
  waiting for transfers between devices  63.7 us (23%)
  matrix products  27.2 us (10%)
  local copies, waits for them, and re-layouts  25 us (9%)
  other arithmetic  16.5 us (6%)
  between operations  14.8 us (5%)
    reduce_scatter x4, waiting for transfers between devices, half_scatter(): lax.psum_scatter(share.astype(jnp.bfloat16), 'tensor', scatter_dimension=...  52.2 us
    psum x1, blocking collectives, shards(): lax.psum(jnp.concatenate([spread.reshape(-1), norm_terms.reshape(-1)]), (...  39.2 us
    all_gather x1, blocking collectives, shards(): lax.all_gather(out_cotangent[0], 'tensor', axis=0, tiled=True)  28.8 us
    all_gather x1, blocking collectives, shards(): lax.all_gather(second_out.astype(bf16), 'tensor', axis=0, tiled=True)  19.5 us
    all_gather x1, blocking collectives, shards(): lax.all_gather(middle_grad.astype(bf16), 'tensor', axis=0, tiled=True)  18.2 us
    unnamed x102, local copies, waits for them, and re-layouts  18 us
    all_gather x1, blocking collectives, shards(): lax.all_gather(first_out.astype(bf16), 'tensor', axis=0, tiled=True)  16.6 us
    all_gather x1, blocking collectives, shards(): lax.all_gather(segment_ids[0], 'tensor', axis=0, tiled=True)  12.6 us
  transfers between devices with their start and end apart: 6, of which 6 were waited for; matrix products, arithmetic and copies ran while one was open for 9% of the time, Pallas kernels for 0%

profile of v1, /device:TPU:0, one launch (start us, length us, event | category | flops | bytes accessed | tf_op | source)
XLA Modules:
  0.0 282.5 jit_solution(11880631662170923697)
XLA Ops:
  7.3 0.9 copy.30
  8.2 0.9 slice_bitcast_fusion.5
  9.1 1.9 concatenate.21
  11.0 12.6 %all-gather = s32[1,512]{1,0:T(1,128)S(1)} all-gather(s32[1,128]{1,0:T(1,128)S(1)} %copy-done.40), channel_id=2, replica_groups=mesh['dp'=8,'tensor'=4] {'tensor'}, dimensions={1}, use_global_device_ids=true | all-gather | bytes 2560 | tf_op jit(solution)/shard_map/all_gather | solution.py:156
  23.7 0.6 slice_reduce_fusion
  24.7 0.9 fusion.9
  25.8 16.6 %all_gather.18 = bf16[512,768]{1,0:T(8,128)(2,1)S(1)} all-gather(bf16[128,768]{1,0:T(8,128)(2,1)S(1)} %fusion.32), channel_id=1, replica_groups=mesh['dp'=8,'tensor'=4] {'tensor'}, dimensions={0}, use_global_device_ids=true | all-gather | bytes 983040 | tf_op jit(solution)/shard_map/all_gather | solution.py:155
  42.4 5.3 %all-gather.4.cloned.1.call-done = bf16[768,2304]{1,0:T(8,128)(2,1)} async-done(((bf16[96,2304]{1,0:T(8,128)(2,1)}), bf16[768,2304]{1,0:T(8,128)(2,1)}) %all-gather.4.cloned.1.call-update) | async-done | bytes 3538960 | tf_op jit(solution)/shard_map/all_gather | solution.py:148
  47.7 1.9 fusion.15
  49.8 0.8 fusion.1
  50.6 0.7 exponential_reduce_fusion
  51.4 0.6 copy-done.31
  52.0 0.9 convolution_convert_fusion.10
  52.9 0.7 copy-done.12
  53.6 2.5 convolution_convert_fusion.6
  56.2 28.8 %all-gather.1 = bf16[1,512,768]{2,1,0:T(8,128)(2,1)} all-gather(bf16[1,128,768]{2,1,0:T(8,128)(2,1)S(1)} %copy-done.10), channel_id=3, replica_groups=mesh['dp'=8,'tensor'=4] {'tensor'}, dimensions={1}, use_global_device_ids=true | all-gather | bytes 983040 | tf_op jit(solution)/shard_map/all_gather | solution.py:157
  85.0 2.9 %reduce-scatter.8.cloned.1.call-done = bf16[128,768]{1,0:T(8,128)(2,1)} async-done(((bf16[512,768]{1,0:T(8,128)(2,1)}), bf16[128,768]{1,0:T(8,128)(2,1)}) %reduce-scatter.8.cloned.1.call-update) | async-done | bytes 196624 | tf_op jit(solution)/shard_map/reduce_scatter | solution.py:123
  87.8 1.1 fusion.53
  88.9 1.1 multiply_reduce_fusion.1
  90.1 1.1 add_convert_fusion.1
  91.1 19.5 %all_gather.21 = bf16[512,768]{1,0:T(8,128)(2,1)S(1)} all-gather(bf16[128,768]{1,0:T(8,128)(2,1)S(1)} %add_convert_fusion.1), channel_id=1, replica_groups=mesh['dp'=8,'tensor'=4] {'tensor'}, dimensions={0}, use_global_device_ids=true | all-gather | bytes 983040 | tf_op jit(solution)/shard_map/all_gather | solution.py:167
  110.6 0.9 copy-done.21
  111.5 2.2 convolution_add_fusion
  114.0 2.0 fusion.63
  116.1 0.9 copy-done.44
  117.0 1.7 convolution_convert_fusion.3
  118.8 3.8 %convolution_convert_fusion.4 = bf16[512,768]{1,0:T(8,128)(2,1)} fusion(bf16[768,2304]{1,0:T(8,128)(2,1)} %all-gather.4.cloned.1.call-done, f32[512,768]{1,0:T(8,128)} %copy-done.46), kind=kOutput, calls=%fused_computation.22 | convolution fusion | flops 607911936 | bytes 3538944 | tf_op jit(solution)/shard_map/dot_general | solution.py:49
  122.7 17.7 %reduce-scatter.12.cloned.1.call-done = bf16[128,768]{1,0:T(8,128)(2,1)} async-done(((bf16[512,768]{1,0:T(8,128)(2,1)}), bf16[128,768]{1,0:T(8,128)(2,1)}) %reduce-scatter.12.cloned.1.call-update) | async-done | bytes 196624 | tf_op jit(solution)/shard_map/reduce_scatter | solution.py:123
  140.4 1.8 fusion.44
  142.2 0.5 broadcast_multiply_fusion.2
  142.7 0.5 broadcast_multiply_fusion.3
  143.3 22.0 %reduce-scatter.10.cloned.1.call-done = bf16[128,768]{1,0:T(8,128)(2,1)} async-done(((bf16[512,768]{1,0:T(8,128)(2,1)}), bf16[128,768]{1,0:T(8,128)(2,1)}) %reduce-scatter.10.cloned.1.call-update) | async-done | bytes 196624 | tf_op jit(solution)/shard_map/reduce_scatter | solution.py:123
  165.3 2.7 fusion.58
  167.9 0.7 copy-done.4
  168.7 18.2 %all_gather.23 = bf16[512,768]{1,0:T(8,128)(2,1)S(1)} all-gather(bf16[128,768]{1,0:T(8,128)(2,1)S(1)} %convert_element_type.111), channel_id=1, replica_groups=mesh['dp'=8,'tensor'=4] {'tensor'}, dimensions={0}, use_global_device_ids=true | all-gather | bytes 983040 | tf_op jit(solution)/shard_map/all_gather | solution.py:180
  186.9 0.9 copy-done.1
  187.9 1.6 convolution_convert_fusion.9
  189.6 1.6 fusion.60
  191.2 1.2 multiply_convert_fusion
  192.5 0.6 convolution_convert_fusion.8
  193.1 0.3 copy-done.15
  193.4 0.5 fusion.61
  193.9 3.1 %convolution_convert_fusion.5 = bf16[512,768]{1,0:T(8,128)(2,1)} fusion(bf16[768,2304]{1,0:T(8,128)(2,1)} %all-gather.4.cloned.1.call-done, bf16[512,192]{0,1:T(8,128)(2,1)S(1)} %bitcast.154, bf16[512,192]{0,1:T(8,128)(2,1)S(1)} %bitcast.147, bf16[512,192]{0,1:T(8,128)(2,1)S(1)} %bitcast.145), kind=kOutput, calls=%fused_computation.23 | convolution fusion | flops 455147520 | bytes 2359296 | tf_op jit(solution)/shard_map/dot_general | solution.py:49
  197.1 0.8 convolution_convert_fusion.1
  198.1 0.5 copy-done.47
  198.7 1.0 fusion.8
  200.2 0.6 convolution_convert_fusion.2
  200.8 2.1 pad_maximum_fusion
  202.9 5.8 %copy.44 = bf16[768,2304]{1,0:T(8,128)(2,1)} copy(bf16[768,2304]{0,1:T(8,128)(2,1)} %pad_maximum_fusion) | data formatting | bytes 7077888
  208.8 0.8 copy-done.11
  210.1 9.6 %reduce-scatter.14.cloned.1.call-done = bf16[128,768]{1,0:T(8,128)(2,1)} async-done(((bf16[512,768]{1,0:T(8,128)(2,1)}), bf16[128,768]{1,0:T(8,128)(2,1)}) %reduce-scatter.14.cloned.1.call-update) | async-done | bytes 196624 | tf_op jit(solution)/shard_map/reduce_scatter | solution.py:123
  219.8 1.2 fusion.45
  221.0 39.2 %psum.7 = f32[9216]{0:T(1024)S(1)} all-reduce(f32[9216]{0:T(1024)S(1)} %pad_maximum_fusion.5), channel_id=1, replica_groups=mesh['dp'=8,'tensor'=4] {'dp','tensor'}, use_global_device_ids=true, to_apply=%region_25.26 | all-reduce | flops 9216 | bytes 73728 | tf_op jit(solution)/shard_map/psum | solution.py:214
  260.4 0.7 reshape.268
  261.0 0.7 dynamic-slice.11
  261.7 0.6 slice.189
  262.3 0.6 slice.191
  262.9 1.9 fusion.36
  264.8 6.1 %reduce-scatter.16.cloned.1.call-done = bf16[96,2304]{1,0:T(8,128)(2,1)} async-done(((bf16[768,2304]{1,0:T(8,128)(2,1)}), bf16[96,2304]{1,0:T(8,128)(2,1)}) %reduce-scatter.16.cloned.1.call-update) | async-done | bytes 442384
  270.8 1.3 copy.45
  272.3 0.7 slice_bitcast_fusion.1
  273.0 0.9 copy.37
  273.8 0.9 copy.38
  274.7 0.9 copy.36
  (138 shorter events, 3.0 us)
Async XLA Ops:
  7.2 3.9 %copy-start.40 = (s32[1,128]{1,0:T(1,128)S(1)}, s32[1,128]{1,0:T(1,128)}, u32[]{:S(2)}) copy-start(s32[1,128]{1,0:T(1,128)} %param.20) | copy-start | bytes 1540
  7.2 16.5 %copy-start.27 = (f32[4,768]{1,0:T(4,128)S(1)}, f32[4,768]{1,0:T(4,128)}, u32[]{:S(2)}) copy-start(f32[4,768]{1,0:T(4,128)} %param.28) | copy-start | bytes 36868
  7.2 16.5 %copy-start.33 = (f32[2,768]{1,0:T(2,128)S(1)}, f32[2,768]{1,0:T(2,128)}, u32[]{:S(2)}) copy-start(f32[2,768]{1,0:T(2,128)} %param.27) | copy-start | bytes 18436
  7.2 17.1 %copy-start = (bf16[1,128,768]{2,1,0:T(8,128)(2,1)S(1)}, bf16[1,128,768]{2,1,0:T(8,128)(2,1)}, u32[]{:S(2)}) copy-start(bf16[1,128,768]{2,1,0:T(8,128)(2,1)} %param.19) | copy-start | bytes 589828
  7.2 17.4 %copy-start.39 = (f32[2,192]{1,0:T(2,128)S(1)}, f32[2,192]{1,0:T(2,128)}, u32[]{:S(2)}) copy-start(f32[2,192]{1,0:T(2,128)} %param.25) | copy-start | bytes 4612
  7.2 40.5 %all-gather.4.cloned.1.call-start = ((), (), s32[]{:S(2)}) async-start(), calls=%async_computation.5 | async-start | bytes 3981312 | tf_op jit(solution)/shard_map/all_gather | solution.py:148
  11.0 76.8 %reduce-scatter.8.cloned.1.call-start = ((), (), s32[]{:S(2)}) async-start(), calls=%async_computation.6 | async-start | bytes 983040 | tf_op jit(solution)/shard_map/reduce_scatter | solution.py:123
  24.4 1.3 copy-start.28
  24.7 1.1 copy-start.34
  42.4 7.3 %copy-start.6 = (bf16[512,768]{1,0:T(8,128)(2,1)}, bf16[512,768]{1,0:T(8,128)(2,1)S(1)}, u32[]{:S(2)}) copy-start(bf16[512,768]{1,0:T(8,128)(2,1)S(1)} %all_gather.18) | copy-start | bytes 2359300
  47.7 2.1 copy-start.8
  49.7 0.9 copy-start.14
  49.8 0.8 copy-start.16
  49.8 1.6 copy-start.23
  51.4 0.6 copy-start.31
  52.9 0.7 copy-start.12
  52.9 3.3 %copy-start.10 = (bf16[1,128,768]{2,1,0:T(8,128)(2,1)S(1)}, bf16[1,128,768]{2,1,0:T(8,128)(2,1)}, u32[]{:S(2)}) copy-start(bf16[1,128,768]{2,1,0:T(8,128)(2,1)} %param.29) | copy-start | bytes 589828
  56.1 84.3 %reduce-scatter.12.cloned.1.call-start = ((), (), s32[]{:S(2)}) async-start(), calls=%async_computation.8 | async-start | bytes 983040 | tf_op jit(solution)/shard_map/reduce_scatter | solution.py:123
  85.0 26.5 %copy-start.41 = (f32[768]{0:T(1024)S(1)}, f32[768]{0:T(1024)}, u32[]{:S(2)}) copy-start(f32[768]{0:T(1024)} %param.26) | copy-start | bytes 9220
  88.9 24.8 %copy-start.30 = (f32[128]{0:T(128)}, f32[128]{0:T(128)S(1)}, u32[]{:S(2)}) copy-start(f32[128]{0:T(128)S(1)} %broadcast_multiply_fusion.4) | copy-start | bytes 1540
  90.1 23.7 %copy-start.36 = (f32[128]{0:T(128)}, f32[128]{0:T(128)S(1)}, u32[]{:S(2)}) copy-start(f32[128]{0:T(128)S(1)} %add_rsqrt_fusion) | copy-start | bytes 1540
  110.6 0.9 copy-start.21
  111.5 2.4 copy-start.18
  111.5 2.6 copy-start.19
  114.0 2.0 copy-start.46
  116.1 0.9 copy-start.44
  118.7 21.7 %copy-start.3 = (bf16[128,768]{1,0:T(8,128)(2,1)S(1)}, bf16[128,768]{1,0:T(8,128)(2,1)}, u32[]{:S(2)}) copy-start(bf16[128,768]{1,0:T(8,128)(2,1)} %reduce-scatter.8.cloned.1.call-done) | copy-start | bytes 589828
  118.7 46.5 %reduce-scatter.10.cloned.1.call-start = ((), (), s32[]{:S(2)}) async-start(), calls=%async_computation.7 | async-start | bytes 983040 | tf_op jit(solution)/shard_map/reduce_scatter | solution.py:123
  122.6 97.1 %reduce-scatter.14.cloned.1.call-start = ((), (), s32[]{:S(2)}) async-start(), calls=%async_computation.9 | async-start | bytes 983040 | tf_op jit(solution)/shard_map/reduce_scatter | solution.py:123
  167.9 0.7 copy-start.4
  167.9 21.5 %copy-start.13 = (bf16[3,64,512]{2,1,0:T(8,128)(2,1)S(1)}, bf16[3,64,512]{2,1,0:T(8,128)(2,1)}, u32[]{:S(2)}) copy-start(bf16[3,64,512]{2,1,0:T(8,128)(2,1)} %copy-done.12) | copy-start | bytes 589828
  168.7 20.9 %copy-start.9 = (pred[512,512]{0,1:T(8,128)(4,1)S(1)}, pred[512,512]{0,1:T(8,128)(4,1)}, u32[]{:S(2)}) copy-start(pred[512,512]{0,1:T(8,128)(4,1)} %fusion.9) | copy-start | bytes 786436
  168.7 20.9 %copy-start.32 = (f32[3,512]{1,0:T(4,128)S(1)}, f32[3,512]{1,0:T(4,128)}, u32[]{:S(2)}) copy-start(f32[3,512]{1,0:T(4,128)} %copy-done.31) | copy-start | bytes 18436
  186.9 0.9 copy-start.1
  189.6 1.6 copy-start.24
  191.2 2.6 copy-start.42
  191.2 1.2 copy-start.17
  192.5 0.9 copy-start.15
  193.9 3.2 %copy-start.22 = (bf16[512,768]{1,0:T(8,128)(2,1)S(1)}, bf16[512,768]{1,0:T(8,128)(2,1)}, u32[]{:S(2)}) copy-start(bf16[512,768]{1,0:T(8,128)(2,1)} %copy-done.21) | copy-start | bytes 2359300
  193.9 3.2 %copy-start.45 = (bf16[512,768]{1,0:T(8,128)(2,1)S(1)}, bf16[512,768]{1,0:T(8,128)(2,1)}, u32[]{:S(2)}) copy-start(bf16[512,768]{1,0:T(8,128)(2,1)} %copy-done.44) | copy-start | bytes 2359300
  197.0 1.1 copy-start.20
  197.0 73.8 %reduce-scatter.16.cloned.1.call-start = ((), (), s32[]{:S(2)}) async-start(), calls=%async_computation.10 | async-start | bytes 3981312
  197.1 1.6 copy-start.47
  198.7 1.1 copy-start.2
  198.7 1.5 copy-start.7
  198.7 1.5 copy-start.43
  208.7 0.9 copy-start.11
  208.7 1.0 copy-start.25
  208.7 1.0 copy-start.26
  208.7 1.1 copy-start.38
  208.7 1.2 copy-start.37
  208.7 11.0 %copy-start.29 = (f32[128]{0:T(128)S(1)}, f32[128]{0:T(128)}, u32[]{:S(2)}) copy-start(f32[128]{0:T(128)} %copy-done.28) | copy-start | bytes 1540
  208.8 11.0 %copy-start.35 = (f32[128]{0:T(128)S(1)}, f32[128]{0:T(128)}, u32[]{:S(2)}) copy-start(f32[128]{0:T(128)} %copy-done.34) | copy-start | bytes 1540
  208.8 54.1 %copy-start.5 = (f32[128,768]{1,0:T(8,128)S(1)}, f32[128,768]{1,0:T(8,128)}, u32[]{:S(2)}) copy-start(f32[128,768]{1,0:T(8,128)} %copy-done.4) | copy-start | bytes 1179652
Sparse Core Ops, SparseCore 0:
  11.1 36.5 all-gather.3
  56.2 31.5 reduce-scatter.7
  118.8 21.4 reduce-scatter.11
  142.5 22.6 reduce-scatter.9
  197.1 22.5 reduce-scatter.13
  223.1 47.6 reduce-scatter.15

commit v2 on v1

--- a/solution.py
+++ b/solution.py
@@ -1,8 +1,11 @@
+import functools
 import math
 
 import jax
 import jax.numpy as jnp
 from jax import lax
+from jax.experimental import pallas as pl
+from jax.experimental.pallas import tpu as pltpu
 from jax.sharding import PartitionSpec as P
 
 HEAD = 64
@@ -231,6 +234,595 @@
     )
 
 
+def matmul(left, right):
+    return jnp.dot(left, right, preferred_element_type=jnp.float32)
+
+
+def layer_kernel(
+    nt,
+    nd,
+    x_ref,
+    seg_ref,
+    wq_ref,
+    wo_ref,
+    wi_ref,
+    wb_ref,
+    cot_ref,
+    qvb_ref,
+    inb_ref,
+    gains_ref,
+    biases_ref,
+    bo_ref,
+    ig_ref,
+    gq_ref,
+    go_ref,
+    gi_ref,
+    gb_ref,
+    sm_ref,
+    fq,
+    fo,
+    fi,
+    fb,
+    first_ref,
+    second_ref,
+    cot_full,
+    mid_full,
+    segs,
+    qs,
+    ks,
+    vs,
+    ctx,
+    probs,
+    hb,
+    act,
+    hh,
+    cg,
+    ph,
+    send,
+    recv,
+    own,
+    mid,
+    norm1,
+    norm2,
+    mgrad,
+    pq,
+    po,
+    pi,
+    pb,
+    aq,
+    ao,
+    ai,
+    ab,
+    bq,
+    bo,
+    bi,
+    bb,
+    rq,
+    ro,
+    ri,
+    rb,
+    small,
+    zsmall,
+    psmall,
+    csmall,
+    csend,
+    zs,
+    zr,
+    ds,
+    dr,
+):
+    bf16 = jnp.bfloat16
+    f32 = jnp.float32
+    nc = nd // 2
+    t = lax.axis_index("tensor")
+    d = lax.axis_index("dp")
+    core = lax.rem(d, 2)
+    chip = d // 2
+    partner = chip * 2 + 1 - core
+    T, D = x_ref.shape
+    rows = wq_ref.shape[0]
+    E = ctx.shape[1]
+    heads = E // HEAD
+    seq = nt * T
+    weights = ((wq_ref, fq), (wo_ref, fo), (wi_ref, fi), (wb_ref, fb))
+    grads = (
+        (pq, aq, bq, rq, gq_ref),
+        (po, ao, bo, ro, go_ref),
+        (pi, ai, bi, ri, gi_ref),
+        (pb, ab, bb, rb, gb_ref),
+    )
+
+    def remote(src, dst, ssem, rsem, **where):
+        return pltpu.make_async_remote_copy(
+            src_ref=src,
+            dst_ref=dst,
+            send_sem=ssem,
+            recv_sem=rsem,
+            device_id=where,
+            device_id_type=pl.DeviceIdType.MESH,
+        )
+
+    def blk(index, size=T):
+        return pl.ds(pl.multiple_of(index * size, size), size)
+
+    def other(k):
+        return lax.rem(t + k, nt)
+
+    def chip_at(k):
+        return lax.rem(chip + k, nc)
+
+    def zcopy(kind, k, src, dst):
+        return remote(src, dst, zs.at[kind, k], zr.at[kind, t], tensor=other(k))
+
+    def zwait(kind, k, dst):
+        remote(dst, dst, zs.at[kind, 0], zr.at[kind, other(k)], tensor=other(k)).wait_recv()
+
+    sent = []
+
+    def go_send(copy):
+        copy.start()
+        sent.append(copy)
+
+    def gather_send(kind, ref):
+        for k in range(1, nt):
+            go_send(zcopy(kind, k, ref.at[blk(t)], ref.at[blk(t)]))
+
+    barrier = pltpu.get_barrier_semaphore()
+    for k in range(1, nt):
+        pl.semaphore_signal(
+            barrier, inc=1, device_id={"tensor": other(k)}, device_id_type=pl.DeviceIdType.MESH
+        )
+    for k in range(1, nc):
+        pl.semaphore_signal(
+            barrier,
+            inc=1,
+            device_id={"dp": chip_at(k) * 2 + core},
+            device_id_type=pl.DeviceIdType.MESH,
+        )
+    pl.semaphore_signal(
+        barrier, inc=1, device_id={"dp": partner}, device_id_type=pl.DeviceIdType.MESH
+    )
+    pl.semaphore_wait(barrier, nt - 1 + nc - 1 + 1)
+
+    def weight_send(w):
+        src, full = weights[w]
+        for k in range(1, nc):
+            go_send(
+                remote(
+                    src,
+                    full.at[blk(d, rows)],
+                    ds.at[0, w, k],
+                    dr.at[0, w, chip],
+                    dp=chip_at(k) * 2 + core,
+                )
+            )
+        go_send(
+            remote(src, full.at[blk(d, rows)], ds.at[1, w, 0], dr.at[1, w, chip], dp=partner)
+        )
+        full[blk(d, rows), :] = src[...]
+
+    def weight_pass(w):
+        full = weights[w][1]
+        for k in range(1, nc):
+            c = chip_at(k)
+            piece = full.at[blk(c * 2 + core, rows)]
+            remote(piece, piece, ds.at[0, w, 0], dr.at[0, w, c], dp=c * 2 + core).wait_recv()
+            go_send(remote(piece, piece, ds.at[1, w, k], dr.at[1, w, c], dp=partner))
+
+    def weight_wait(w):
+        full = weights[w][1]
+        for k in range(nc):
+            c = chip_at(k)
+            piece = full.at[blk(c * 2 + 1 - core, rows)]
+            remote(piece, piece, ds.at[1, w, 0], dr.at[1, w, c], dp=partner).wait_recv()
+
+    weight_send(0)
+    residual = x_ref[...].astype(f32)
+    first_out, normed_first, inv_first = normalize(residual, gains_ref[0:1], biases_ref[0:1])
+    norm1[...] = normed_first
+    first_ref[blk(t), :] = first_out.astype(bf16)
+    gather_send(0, first_ref)
+    segs[t] = seg_ref[...]
+    for k in range(1, nt):
+        go_send(zcopy(1, k, seg_ref, segs.at[t]))
+    for w in (1, 2, 3):
+        weight_send(w)
+    cot_full[blk(t), :] = cot_ref[...]
+    for k in range(1, nt):
+        go_send(zcopy(2, k, cot_ref, cot_full.at[blk(t)]))
+    weight_pass(0)
+    weight_wait(0)
+
+    def project(s, carry):
+        b = other(s)
+
+        @pl.when(s > 0)
+        def _():
+            zwait(0, s, first_ref.at[blk(b)])
+
+        out = matmul(first_ref[blk(b), :], fq[...])
+        qs[blk(b), :] = (out[:, :E] + qvb_ref[0:1]).astype(bf16)
+        ks[blk(b), :] = out[:, E : 2 * E].astype(bf16)
+        vs[blk(b), :] = (out[:, 2 * E :] + qvb_ref[1:2]).astype(bf16)
+        return carry
+
+    lax.fori_loop(0, nt, project, 0)
+    for k in range(1, nt):
+        zwait(1, k, segs.at[other(k)])
+    weight_pass(1)
+
+    reach = (seq // 2 - 1 + T - 1) // T
+    inv_root = 1.0 / math.sqrt(HEAD)
+    for b in range(nt):
+        low = max(0, b - reach)
+        width = (b + 1 - low) * T
+        key_seg = jnp.concatenate(
+            [segs[j][0:1].astype(f32) for j in range(low, b + 1)], axis=1
+        )
+        query_seg = jnp.transpose(jnp.broadcast_to(segs[b][0:1].astype(f32), (T, T)))[:, 0:1]
+        query_pos = lax.broadcasted_iota(jnp.int32, (T, width), 0) + b * T
+        key_pos = lax.broadcasted_iota(jnp.int32, (T, width), 1) + low * T
+        allowed = (key_pos <= query_pos) & (query_seg == key_seg)
+        for h in range(heads):
+            cols = slice(h * HEAD, (h + 1) * HEAD)
+            scores = (
+                contract_cols(qs[b * T : (b + 1) * T, cols], ks[low * T : (b + 1) * T, cols])
+                * inv_root
+            )
+            scores = jnp.where(allowed, scores, -jnp.inf)
+            row_max = jnp.max(scores, axis=-1, keepdims=True)
+            log_total = row_max + jnp.log(
+                jnp.sum(jnp.exp(scores - row_max), axis=-1, keepdims=True)
+            )
+            prob = jnp.exp(scores - log_total)
+            probs[h, b, :, :width] = prob
+            ctx[b * T : (b + 1) * T, cols] = matmul(
+                prob.astype(bf16), vs[low * T : (b + 1) * T, cols]
+            ).astype(bf16)
+    weight_wait(1)
+
+    def scatter(kind, slot, make):
+        def step(s, carry):
+            b = other(s + 1)
+            share = make(b)
+
+            @pl.when(s < nt - 1)
+            def _():
+                send[slot, b] = share.astype(bf16)
+                zcopy(kind, s + 1, send.at[slot, b], recv.at[slot, t]).start()
+
+            @pl.when(s == nt - 1)
+            def _():
+                own[slot] = share
+
+            return carry
+
+        lax.fori_loop(0, nt, step, 0)
+        for k in range(1, nt):
+            sent.append(zcopy(kind, k, send.at[slot, other(k)], recv.at[slot, t]))
+
+    def scattered(kind, slot):
+        total = own[slot]
+        for k in range(1, nt):
+            zwait(kind, k, recv.at[slot, other(k)])
+            total = total + recv[slot, other(k)].astype(f32)
+        return total
+
+    scatter(5, 0, lambda b: contract_cols(ctx[blk(b), :], fo[...]))
+    weight_pass(2)
+    weight_pass(3)
+    weight_wait(3)
+    middle = residual + scattered(5, 0) + biases_ref[2:3]
+    mid[...] = middle
+    second_out, normed_second, inv_second = normalize(middle, gains_ref[1:2], biases_ref[1:2])
+    norm2[...] = normed_second
+    second_ref[blk(t), :] = second_out.astype(bf16)
+    gather_send(3, second_ref)
+
+    def back_step(s, carry):
+        b = other(s)
+
+        @pl.when(s > 0)
+        def _():
+            zwait(2, s, cot_full.at[blk(b)])
+
+        hb[blk(b), :] = matmul(cot_full[blk(b), :], fb[...])
+        return carry
+
+    lax.fori_loop(0, nt, back_step, 0)
+    weight_wait(2)
+    small[...] = jnp.zeros_like(small)
+
+    def hidden_step(s, carry):
+        b = other(s)
+
+        @pl.when(s > 0)
+        def _():
+            zwait(3, s, second_ref.at[blk(b)])
+
+        pre = matmul(second_ref[blk(b), :], fi[...]) + inb_ref[...]
+        value, slope = gelu_pair(pre)
+        act[blk(b), :] = value.astype(bf16)
+        grad = hb[blk(b), :] * slope
+        small[8:9, : grad.shape[1]] += jnp.sum(grad, axis=0, keepdims=True)
+        half = grad.astype(bf16)
+        hh[blk(b), :] = half
+        share = contract_cols(half, fi[...])
+
+        @pl.when(s > 0)
+        def _():
+            send[1, b] = share.astype(bf16)
+            zcopy(6, s, send.at[1, b], recv.at[1, t]).start()
+
+        @pl.when(s == 0)
+        def _():
+            own[1] = share
+
+        return carry
+
+    lax.fori_loop(0, nt, hidden_step, 0)
+    for k in range(1, nt):
+        sent.append(zcopy(6, k, send.at[1, other(k)], recv.at[1, t]))
+    scatter(7, 2, lambda b: contract_cols(act[blk(b), :], fb[...]))
+
+    def weight_grad(w, left, right):
+        part, first_recv = grads[w][0], grads[w][1]
+        step = 128
+
+        def chunk(c, carry):
+            part[blk(c, step), :] = contract_rows(left[:, blk(c, step)], right[...]).astype(bf16)
+            return carry
+
+        lax.fori_loop(0, D // step, chunk, 0)
+        for c in range(nc):
+            go_send(
+                remote(
+                    part.at[blk(c * 2 + 1 - core, rows)],
+                    first_recv.at[c],
+                    ds.at[2, w, c],
+                    dr.at[2, w, c],
+                    dp=partner,
+                )
+            )
+
+    def pair_sum(w, c):
+        part, first_recv = grads[w][0], grads[w][1]
+        piece = first_recv.at[c]
+        remote(piece, piece, ds.at[2, w, 0], dr.at[2, w, c], dp=partner).wait_recv()
+        return part[blk(c * 2 + core, rows), :].astype(f32) + first_recv[c].astype(f32)
+
+    def grad_pass(w):
+        pairs, second_recv, out = grads[w][2], grads[w][3], grads[w][4]
+        for k in range(1, nc):
+            c = chip_at(k)
+            pairs[c] = pair_sum(w, c).astype(bf16)
+            go_send(
+                remote(
+                    pairs.at[c],
+                    second_recv.at[chip],
+                    ds.at[3, w, k],
+                    dr.at[3, w, chip],
+                    dp=c * 2 + core,
+                )
+            )
+        out[...] = pair_sum(w, chip)
+
+    def grad_finish(w):
+        second_recv, out = grads[w][3], grads[w][4]
+        total = out[...]
+        for k in range(1, nc):
+            c = chip_at(k)
+            piece = second_recv.at[c]
+            remote(piece, piece, ds.at[3, w, 0], dr.at[3, w, c], dp=c * 2 + core).wait_recv()
+            total = total + second_recv[c].astype(f32)
+        out[...] = total
+
+    weight_grad(2, second_ref, hh)
+    second_grad = scattered(6, 1)
+    cotangent = cot_ref[...].astype(f32)
+    middle_grad = cotangent + normalize_back(second_grad, norm2[...], inv_second, gains_ref[1:2])
+    mgrad[...] = middle_grad
+    mid_full[blk(t), :] = middle_grad.astype(bf16)
+    gather_send(4, mid_full)
+    small[1:2, :] = jnp.sum(second_grad * norm2[...], axis=0, keepdims=True)
+    small[3:4, :] = jnp.sum(second_grad, axis=0, keepdims=True)
+    small[4:5, :] = jnp.sum(middle_grad, axis=0, keepdims=True)
+    small[5:6, :] = jnp.sum(cotangent, axis=0, keepdims=True)
+    weight_grad(3, cot_full, act)
+    grad_pass(2)
+    grad_pass(3)
+    bo_ref[...] = (mid[...] + scattered(7, 2) + biases_ref[3:4]).astype(bf16)
+
+    def context_step(s, carry):
+        b = other(s)
+
+        @pl.when(s > 0)
+        def _():
+            zwait(4, s, mid_full.at[blk(b)])
+
+        cg[blk(b), :] = matmul(mid_full[blk(b), :], fo[...]).astype(bf16)
+        return carry
+
+    lax.fori_loop(0, nt, context_step, 0)
+
+    for h in range(heads):
+        cols = slice(h * HEAD, (h + 1) * HEAD)
+        key_grads = [None] * nt
+        value_grads = [None] * nt
+        query_sum = 0.0
+        for b in range(nt):
+            low = max(0, b - reach)
+            width = (b + 1 - low) * T
+            here, window = slice(b * T, (b + 1) * T), slice(low * T, (b + 1) * T)
+            prob = probs[h, b, :, :width]
+            grad = cg[here, cols]
+            prob_grad = contract_cols(grad, vs[window, cols])
+            row_dot = jnp.sum(
+                grad.astype(f32) * ctx[here, cols].astype(f32), axis=-1, keepdims=True
+            )
+            score_grad = (prob * (prob_grad - row_dot) * inv_root).astype(bf16)
+            query_grad = matmul(score_grad, ks[window, cols])
+            query_sum = query_sum + jnp.sum(query_grad, axis=0, keepdims=True)
+            ph[here, h * HEAD : (h + 1) * HEAD] = query_grad.astype(bf16)
+            key_part = contract_rows(score_grad, qs[here, cols])
+            value_part = contract_rows(prob.astype(bf16), grad)
+            for j in range(low, b + 1):
+                at = slice((j - low) * T, (j - low + 1) * T)
+                fresh = key_grads[j] is None
+                key_grads[j] = key_part[at] if fresh else key_grads[j] + key_part[at]
+                value_grads[j] = value_part[at] if fresh else value_grads[j] + value_part[at]
+        value_sum = 0.0
+        for j in range(nt):
+            here = slice(j * T, (j + 1) * T)
+            ph[here, E + h * HEAD : E + (h + 1) * HEAD] = key_grads[j].astype(bf16)
+            ph[here, 2 * E + h * HEAD : 2 * E + (h + 1) * HEAD] = value_grads[j].astype(bf16)
+            value_sum = value_sum + jnp.sum(value_grads[j], axis=0, keepdims=True)
+        small[9:10, h * HEAD : (h + 1) * HEAD] = query_sum
+        small[10:11, h * HEAD : (h + 1) * HEAD] = value_sum
+
+    scatter(8, 3, lambda b: contract_cols(ph[blk(b), :], fq[...]))
+    weight_grad(0, first_ref, ph)
+    weight_grad(1, mid_full, ctx)
+    grad_pass(0)
+    grad_pass(1)
+    first_grad = scattered(8, 3)
+    ig_ref[...] = mgrad[...] + normalize_back(
+        first_grad, norm1[...], inv_first, gains_ref[0:1]
+    )
+    small[0:1, :] = jnp.sum(first_grad * norm1[...], axis=0, keepdims=True)
+    small[2:3, :] = jnp.sum(first_grad, axis=0, keepdims=True)
+    zsmall[t] = small[0:8, :]
+    for k in range(1, nt):
+        go_send(zcopy(9, k, zsmall.at[t], zsmall.at[t]))
+    for w in (2, 3):
+        grad_finish(w)
+    summed = small[0:8, :]
+    for k in range(1, nt):
+        zwait(9, k, zsmall.at[other(k)])
+    summed = zsmall[0]
+    for k in range(1, nt):
+        summed = summed + zsmall[k]
+    psmall[core] = jnp.concatenate([summed, small[8:16, :]], axis=0)
+    go_send(
+        remote(psmall.at[core], psmall.at[core], ds.at[2, 4, 0], dr.at[2, 4, 0], dp=partner)
+    )
+    piece = psmall.at[1 - core]
+    remote(piece, piece, ds.at[2, 4, 1], dr.at[2, 4, 0], dp=partner).wait_recv()
+    csmall[chip] = psmall[0] + psmall[1]
+    for k in range(1, nc):
+        go_send(
+            remote(
+                csmall.at[chip],
+                csmall.at[chip],
+                ds.at[3, 4, k],
+                dr.at[3, 4, chip],
+                dp=chip_at(k) * 2 + core,
+            )
+        )
+    for w in (0, 1):
+        grad_finish(w)
+    for k in range(1, nc):
+        c = chip_at(k)
+        piece = csmall.at[c]
+        remote(piece, piece, ds.at[3, 4, 0], dr.at[3, 4, c], dp=c * 2 + core).wait_recv()
+    total = csmall[0]
+    for c in range(1, nc):
+        total = total + csmall[c]
+    sm_ref[...] = total
+    for copy in sent:
+        copy.wait_send()
+
+
+def kernel_shards(
+    nt,
+    nd,
+    block_input,
+    segment_ids,
+    w_qkv,
+    w_out,
+    w_in,
+    w_back,
+    qv_bias,
+    in_bias,
+    norm_gains,
+    norm_biases,
+    out_cotangent,
+):
+    bf16, f32 = jnp.bfloat16, jnp.float32
+    T, D = block_input.shape[1:]
+    E, F = w_qkv.shape[2], w_in.shape[1]
+    rows = D // nd
+    seq = nt * T
+    heads = E // HEAD
+    nc = nd // 2
+    reach = (seq // 2 - 1 + T - 1) // T
+    window = min(nt, reach + 1) * T
+    widths = (3 * E, E, F, F)
+    wq = jnp.concatenate([w_qkv[0], w_qkv[1], w_qkv[2]], axis=1)
+    seg = jnp.broadcast_to(segment_ids, (8, T))
+    vm = pltpu.VMEM
+    scratch = (
+        [vm((D, n), bf16) for n in widths]
+        + [vm((seq, D), bf16)] * 4
+        + [vm((nt, 8, T), jnp.int32)]
+        + [vm((seq, E), bf16)] * 4
+        + [vm((heads, nt, T, window), f32)]
+        + [vm((seq, F), f32), vm((seq, F), bf16), vm((seq, F), bf16)]
+        + [vm((seq, E), bf16), vm((seq, 3 * E), bf16)]
+        + [vm((4, nt, T, D), bf16)] * 2
+        + [vm((4, T, D), f32)]
+        + [vm((T, D), f32)] * 4
+        + [vm((D, n), bf16) for n in widths]
+        + [vm((nc, rows, n), bf16) for n in widths] * 3
+        + [vm((16, D), f32), vm((nt, 8, D), f32), vm((2, 16, D), f32), vm((nc, 16, D), f32)]
+        + [vm((8, 128), f32)]
+        + [pltpu.SemaphoreType.DMA((10, nt))] * 2
+        + [pltpu.SemaphoreType.DMA((4, 5, nc))] * 2
+    )
+    spec = pl.BlockSpec(memory_space=pltpu.VMEM)
+    outs = pl.pallas_call(
+        functools.partial(layer_kernel, nt, nd),
+        out_shape=[
+            jax.ShapeDtypeStruct((T, D), bf16),
+            jax.ShapeDtypeStruct((T, D), f32),
+            *[jax.ShapeDtypeStruct((rows, n), f32) for n in widths],
+            jax.ShapeDtypeStruct((16, D), f32),
+        ],
+        in_specs=[spec] * 11,
+        out_specs=[spec] * 7,
+        scratch_shapes=scratch,
+        compiler_params=pltpu.CompilerParams(
+            collective_id=0, has_side_effects=True, vmem_limit_bytes=60 * 1024 * 1024
+        ),
+        name="layer",
+    )(
+        block_input[0],
+        seg,
+        wq,
+        w_out.T,
+        w_in,
+        w_back.T,
+        out_cotangent[0],
+        qv_bias,
+        in_bias[None],
+        norm_gains,
+        norm_biases,
+    )
+    block_out, input_grad, gq, go, gi, gb, total = outs
+    return (
+        block_out[None],
+        input_grad[None],
+        jnp.stack([gq[:, :E], gq[:, E : 2 * E], gq[:, 2 * E :]]),
+        go.T,
+        gi,
+        gb.T,
+        total[9:11, :E],
+        total[8, :F],
+        total[:2],
+        total[2:6],
+    )
+
+
 def solution(mesh):
     in_specs = (
         P("dp", "tensor", None),
@@ -257,4 +849,21 @@
         P(),
         P(),
     )
-    return jax.shard_map(shards, mesh=mesh, in_specs=in_specs, out_specs=out_specs, check_vma=False)
+    nt, nd = mesh.shape["tensor"], mesh.shape["dp"]
+
+    def body(*args):
+        block_input, w_qkv, w_in = args[0], args[2], args[4]
+        tokens, features = block_input.shape[1:]
+        fits = (
+            nd % 2 == 0
+            and w_in.shape[0] % 16 == 0
+            and tokens % 128 == 0
+            and features % 128 == 0
+            and w_in.shape[1] <= features
+            and w_qkv.shape[2] % HEAD == 0
+        )
+        if fits:
+            return kernel_shards(nt, nd, *args)
+        return shards(*args)
+
+    return jax.shard_map(body, mesh=mesh, in_specs=in_specs, out_specs=out_specs, check_vma=False)

time: 283 us -> 182 us (0.64)
  Pallas kernels: 0 us -> 164 us
  blocking collectives: 135 us -> 0 us
  waiting for transfers between devices: 63.7 us -> 0 us
  matrix products: 27.2 us -> 0 us
  other arithmetic: 16.5 us -> 1.48 us
  between operations: 14.8 us -> 0.7 us
  local copies, waits for them, and re-layouts: 25 us -> 15.2 us
    pallas_call x0 -> x1, Pallas kernels: none -> 164 us  [kernel_shards(): pl.pallas_call(functools.partial(layer_kernel, nt, nd), out_shape=[jax.Sh...]
    all_gather x5 -> x0, blocking collectives: 95.7 us -> none  [the longest x1 28.8 us: shards(): lax.all_gather(out_cotangent[0], 'tensor', axis=0, tiled=True)]
    reduce_scatter x4 -> x0, waiting for transfers between devices: 52.2 us -> none  [half_scatter(): lax.psum_scatter(share.astype(jnp.bfloat16), 'tensor', scatter_dimension=...]
    psum x1 -> x0, blocking collectives: 39.2 us -> none  [shards(): lax.psum(jnp.concatenate([spread.reshape(-1), norm_terms.reshape(-1)]), (...]
    dot_general x18 -> x0, matrix products: 27.2 us -> none  [the longest x4 11.1 us: contract_cols(): lax.dot_general(left, right, (((1,), (1,)), ((), ())), preferred_element_...]
    unnamed x102 -> x20, local copies, waits for them, and re-layouts: 18 us -> 7.75 us
    reduce_sum x10 -> x0, other arithmetic: 8.99 us -> none  [the longest x1 2.68 us: shards(): jnp.sum(middle_grad, axis=0)]
    unnamed x7 -> x0, waiting for transfers between devices: 6.17 us -> none
  transfers between devices with their start and end apart: 6 -> 0, of which waited for: 6 -> 0; matrix products, arithmetic and copies ran while one was open for 9% -> 0% of each run, Pallas kernels for 0% -> 0%
where the time goes in v2:
time: 182 us; the launch traced here: 181 us
  Pallas kernels  164 us (90%)
  local copies, waits for them, and re-layouts  15.2 us (8%)
    pallas_call x1, Pallas kernels, kernel_shards(): pl.pallas_call(functools.partial(layer_kernel, nt, nd), out_shape=[jax.Sh...  164 us
    unnamed x20, local copies, waits for them, and re-layouts  7.75 us

profile of v2, /device:TPU:0, one launch (start us, length us, event | category | flops | bytes accessed | tf_op | source)
XLA Modules:
  0.0 181.3 jit_solution(13121945726821183144)
XLA Ops:
  0.6 0.0 copy-start.5
  0.7 0.7 copy-done.5
  1.3 0.0 copy-start.6
  1.3 0.6 broadcast_in_dim.18.inb_ref
  1.9 0.1 copy-done.6
  2.0 0.6 broadcast_in_dim.17.seg_ref
  2.6 1.5 copy.21
  4.1 0.9 slice_bitcast_fusion.5
  5.0 0.7 pad_maximum_fusion.1.wq_ref
  5.7 164.0 %layer.1 = (bf16[128,768]{1,0:T(8,128)(2,1)}, f32[128,768]{1,0:T(8,128)}, f32[96,576]{1,0:T(8,128)}, f32[96,192]{1,0:T(8,128)}, f32[96,768]{1,0:T(8,128)}, /*index=5*/f32[96,768]{1,0:T(8,128)}, f32[16,768]{1,0:T(8,128)}) custom-call(bf16[128,768]{1,0:T(8,128)(2,1)} %bitcast.24, s32[8,128]{1,0:T(8,128)} %broadcast_in_dim.17.seg_ref, ...), custom_call_target="tpu_custom_call" | custom-call | tf_op jit(solution)/shard_map/layer/pallas_call | solution.py:783
  169.7 0.0 copy-start.1
  169.7 1.3 slice.36
  171.0 1.3 slice_reduce_fusion
  172.3 1.3 slice.38
  173.7 1.3 slice.39
  175.0 1.6 copy.22
  176.6 0.0 copy-done.1
  176.6 0.1 slice_bitcast_fusion.2
  176.7 0.0 copy-start.4
  176.7 0.0 copy-start
  176.7 0.7 pad_maximum_fusion
  177.5 0.3 copy-done.4
  177.8 0.7 copy.27
  178.4 0.0 copy-done
  178.4 0.0 copy-start.3
  178.4 0.7 copy.28
  179.2 0.4 copy-done.3
  179.5 0.0 copy-start.2
  179.5 0.7 copy.29
  180.3 0.4 copy-done.2
  180.6 0.7 copy.30
Async XLA Ops:
  0.6 0.7 copy-start.5
  1.3 0.7 copy-start.6
  169.7 7.0 %copy-start.1 = (f32[96,576]{1,0:T(8,128)S(1)}, f32[96,576]{1,0:T(8,128)}, u32[]{:S(2)}) copy-start(f32[96,576]{1,0:T(8,128)} %get-tuple-element.19) | copy-start | bytes 663556
  176.7 1.0 copy-start.4
  176.7 1.7 copy-start
  178.4 1.1 copy-start.3
  179.5 1.1 copy-start.2

commit v3 on v2

--- a/solution.py
+++ b/solution.py
@@ -258,7 +258,10 @@
     go_ref,
     gi_ref,
     gb_ref,
-    sm_ref,
+    gqv_ref,
+    ginb_ref,
+    ggain_ref,
+    gbias_ref,
     fq,
     fo,
     fi,
@@ -305,7 +308,9 @@
     zsmall,
     psmall,
     csmall,
-    csend,
+    oq,
+    oo,
+    ob,
     zs,
     zr,
     ds,
@@ -326,10 +331,10 @@
     seq = nt * T
     weights = ((wq_ref, fq), (wo_ref, fo), (wi_ref, fi), (wb_ref, fb))
     grads = (
-        (pq, aq, bq, rq, gq_ref),
-        (po, ao, bo, ro, go_ref),
+        (pq, aq, bq, rq, oq),
+        (po, ao, bo, ro, oo),
         (pi, ai, bi, ri, gi_ref),
-        (pb, ab, bb, rb, gb_ref),
+        (pb, ab, bb, rb, ob),
     )
 
     def remote(src, dst, ssem, rsem, **where):
@@ -563,7 +568,6 @@
     lax.fori_loop(0, nt, hidden_step, 0)
     for k in range(1, nt):
         sent.append(zcopy(6, k, send.at[1, other(k)], recv.at[1, t]))
-    scatter(7, 2, lambda b: contract_cols(act[blk(b), :], fb[...]))
 
     def weight_grad(w, left, right):
         part, first_recv = grads[w][0], grads[w][1]
@@ -615,7 +619,15 @@
             piece = second_recv.at[c]
             remote(piece, piece, ds.at[3, w, 0], dr.at[3, w, c], dp=c * 2 + core).wait_recv()
             total = total + second_recv[c].astype(f32)
-        out[...] = total
+        if w == 0:
+            for c in range(3):
+                gq_ref[c] = total[:, c * E : (c + 1) * E]
+        elif w == 1:
+            go_ref[...] = jnp.transpose(total)
+        elif w == 2:
+            gi_ref[...] = total
+        else:
+            gb_ref[...] = total
 
     weight_grad(2, second_ref, hh)
     second_grad = scattered(6, 1)
@@ -629,9 +641,9 @@
     small[4:5, :] = jnp.sum(middle_grad, axis=0, keepdims=True)
     small[5:6, :] = jnp.sum(cotangent, axis=0, keepdims=True)
     weight_grad(3, cot_full, act)
+    scatter(7, 2, lambda b: contract_cols(act[blk(b), :], fb[...]))
     grad_pass(2)
     grad_pass(3)
-    bo_ref[...] = (mid[...] + scattered(7, 2) + biases_ref[3:4]).astype(bf16)
 
     def context_step(s, carry):
         b = other(s)
@@ -685,6 +697,9 @@
     weight_grad(1, mid_full, ctx)
     grad_pass(0)
     grad_pass(1)
+    bo_ref[...] = (mid[...] + scattered(7, 2) + biases_ref[3:4]).astype(bf16)
+    for w in (2, 3):
+        grad_finish(w)
     first_grad = scattered(8, 3)
     ig_ref[...] = mgrad[...] + normalize_back(
         first_grad, norm1[...], inv_first, gains_ref[0:1]
@@ -694,9 +709,6 @@
     zsmall[t] = small[0:8, :]
     for k in range(1, nt):
         go_send(zcopy(9, k, zsmall.at[t], zsmall.at[t]))
-    for w in (2, 3):
-        grad_finish(w)
-    summed = small[0:8, :]
     for k in range(1, nt):
         zwait(9, k, zsmall.at[other(k)])
     summed = zsmall[0]
@@ -728,7 +740,10 @@
     total = csmall[0]
     for c in range(1, nc):
         total = total + csmall[c]
-    sm_ref[...] = total
+    gqv_ref[...] = total[9:11, :E]
+    ginb_ref[...] = total[8:9, : inb_ref.shape[1]]
+    ggain_ref[...] = total[0:2]
+    gbias_ref[...] = total[2:6]
     for copy in sent:
         copy.wait_send()
 
@@ -775,7 +790,7 @@
         + [vm((D, n), bf16) for n in widths]
         + [vm((nc, rows, n), bf16) for n in widths] * 3
         + [vm((16, D), f32), vm((nt, 8, D), f32), vm((2, 16, D), f32), vm((nc, 16, D), f32)]
-        + [vm((8, 128), f32)]
+        + [vm((rows, n), f32) for n in (3 * E, E, F)]
         + [pltpu.SemaphoreType.DMA((10, nt))] * 2
         + [pltpu.SemaphoreType.DMA((4, 5, nc))] * 2
     )
@@ -785,11 +800,17 @@
         out_shape=[
             jax.ShapeDtypeStruct((T, D), bf16),
             jax.ShapeDtypeStruct((T, D), f32),
-            *[jax.ShapeDtypeStruct((rows, n), f32) for n in widths],
-            jax.ShapeDtypeStruct((16, D), f32),
+            jax.ShapeDtypeStruct((3, rows, E), f32),
+            jax.ShapeDtypeStruct((E, rows), f32),
+            jax.ShapeDtypeStruct((rows, F), f32),
+            jax.ShapeDtypeStruct((rows, F), f32),
+            jax.ShapeDtypeStruct((2, E), f32),
+            jax.ShapeDtypeStruct((1, F), f32),
+            jax.ShapeDtypeStruct((2, D), f32),
+            jax.ShapeDtypeStruct((4, D), f32),
         ],
         in_specs=[spec] * 11,
-        out_specs=[spec] * 7,
+        out_specs=[spec] * 10,
         scratch_shapes=scratch,
         compiler_params=pltpu.CompilerParams(
             collective_id=0, has_side_effects=True, vmem_limit_bytes=60 * 1024 * 1024
@@ -808,19 +829,8 @@
         norm_gains,
         norm_biases,
     )
-    block_out, input_grad, gq, go, gi, gb, total = outs
-    return (
-        block_out[None],
-        input_grad[None],
-        jnp.stack([gq[:, :E], gq[:, E : 2 * E], gq[:, 2 * E :]]),
-        go.T,
-        gi,
-        gb.T,
-        total[9:11, :E],
-        total[8, :F],
-        total[:2],
-        total[2:6],
-    )
+    block_out, input_grad, gq, go, gi, gb, gqv, ginb, ggain, gbias = outs
+    return (block_out[None], input_grad[None], gq, go, gi, gb.T, gqv, ginb[0], ggain, gbias)
 
 
 def solution(mesh):

time: 182 us -> 175 us (0.962)
  Pallas kernels: 164 us -> 160 us
  local copies, waits for them, and re-layouts: 15.2 us -> 12.2 us
    slice x4 -> x0, local copies, waits for them, and re-layouts: 5.33 us -> none  [the longest x1 1.34 us: kernel_shards(): total[8, :F]]
    pallas_call x1, Pallas kernels: 164 us -> 160 us  [kernel_shards(): pl.pallas_call(functools.partial(layer_kernel, nt, nd), out_shape=[jax.Sh...]
    unnamed x20 -> x30, local copies, waits for them, and re-layouts: 7.75 us -> 10.2 us
where the time goes in v3:
time: 175 us
  Pallas kernels  160 us (91%)
  local copies, waits for them, and re-layouts  12.2 us (7%)
  other arithmetic  2.07 us (1%)
    pallas_call x1, Pallas kernels, kernel_shards(): pl.pallas_call(functools.partial(layer_kernel, nt, nd), out_shape=[jax.Sh...  160 us
    unnamed x30, local copies, waits for them, and re-layouts  10.2 us

profile of v3, /device:TPU:0, one launch (start us, length us, event | category | flops | bytes accessed | tf_op | source)
XLA Modules:
  0.0 174.5 jit_solution(18087405434380164805)
XLA Ops:
  0.6 0.0 copy-start.7
  0.7 0.7 copy-done.7
  1.3 0.0 copy-start.9
  1.3 0.6 broadcast_in_dim.18.inb_ref
  1.9 0.1 copy-done.9
  2.0 0.6 broadcast_in_dim.17.seg_ref
  2.6 1.5 copy.21
  4.1 0.9 slice_bitcast_fusion.2
  5.0 0.7 pad_maximum_fusion.wq_ref
  5.7 159.6 %layer.1 = (bf16[128,768]{1,0:T(8,128)(2,1)}, f32[128,768]{1,0:T(8,128)}, f32[3,96,192]{2,1,0:T(8,128)}, f32[192,96]{1,0:T(8,128)}, f32[96,768]{1,0:T(8,128)}, /...) custom-call(bf16[128,768]{1,0:T(8,128)(2,1)} %bitcast.17, ...), custom_call_target="tpu_custom_call" | custom-call | tf_op jit(solution)/shard_map/layer/pallas_call | solution.py:798
  165.3 0.0 copy-start
  165.3 1.3 reduce
  166.6 1.6 copy.31
  168.3 0.0 copy-done
  168.3 0.0 copy-start.3
  168.3 0.7 copy.32
  169.0 0.4 copy-done.3
  169.4 0.0 copy-start.4
  169.4 0.0 copy-start.2
  169.4 0.7 copy.33
  170.1 0.2 copy-done.4
  170.3 0.6 copy.34
  171.0 0.0 copy-done.2
  171.0 0.0 copy-start.1
  171.0 0.7 copy.35
  171.7 0.4 copy-done.1
  172.0 0.0 copy-start.8
  172.0 0.0 copy-start.6
  172.0 0.7 copy.36
  172.8 0.0 copy-done.8
  172.8 0.0 copy-start.5
  172.8 0.6 copy.37
  173.3 0.0 copy-done.6
  173.3 0.6 copy.38
  173.9 0.0 copy-done.5
  173.9 0.6 copy.39
Async XLA Ops:
  0.6 0.7 copy-start.7
  1.3 0.7 copy-start.9
  165.3 3.0 %copy-start = (f32[128,768]{1,0:T(8,128)S(1)}, f32[128,768]{1,0:T(8,128)}, u32[]{:S(2)}) copy-start(f32[128,768]{1,0:T(8,128)} %get-tuple-element.21) | copy-start | bytes 1179652
  168.3 1.1 copy-start.3
  169.4 1.0 copy-start.4
  169.4 1.6 copy-start.2
  171.0 1.1 copy-start.1
  172.0 0.7 copy-start.8
  172.0 1.3 copy-start.6
  172.8 1.2 copy-start.5

commit v4 on v3

--- a/solution.py
+++ b/solution.py
@@ -368,9 +368,59 @@
         copy.start()
         sent.append(copy)
 
+    def line_copy(kind, slot, ref, b, to):
+        piece = ref.at[blk(b)]
+        return remote(piece, piece, zs.at[kind, slot], zr.at[kind, b], tensor=to)
+
+    def line_own(kind, ref, act_on):
+        for slot, to in ((0, t + 1), (2 * nt - 1, t - 1)):
+
+            @pl.when((to >= 0) & (to < nt))
+            def _():
+                act_on(line_copy(kind, slot, ref, t, to))
+
+    def line_place(s):
+        sign = 2 * lax.rem(s, 2) - 1
+        return t + sign * ((s + 1) // 2), t - sign
+
     def gather_send(kind, ref):
-        for k in range(1, nt):
-            go_send(zcopy(kind, k, ref.at[blk(t)], ref.at[blk(t)]))
+        line_own(kind, ref, lambda copy: copy.start())
+
+    def gather_each(kind, ref, work):
+        def step(s, carry):
+            b, to = line_place(s)
+
+            @pl.when((b >= 0) & (b < nt))
+            def _():
+                @pl.when(s > 0)
+                def _():
+                    remote(
+                        ref.at[blk(b)], ref.at[blk(b)], zs.at[kind, 0], zr.at[kind, b], tensor=b
+                    ).wait_recv()
+
+                    @pl.when((to >= 0) & (to < nt))
+                    def _():
+                        line_copy(kind, s, ref, b, to).start()
+
+                work(b, s)
+
+            return carry
+
+        lax.fori_loop(0, 2 * nt - 1, step, 0)
+
+    def gather_drain(kind, ref):
+        line_own(kind, ref, lambda copy: copy.wait_send())
+
+        def step(s, carry):
+            b, to = line_place(s)
+
+            @pl.when((b >= 0) & (b < nt) & (to >= 0) & (to < nt))
+            def _():
+                line_copy(kind, s, ref, b, to).wait_send()
+
+            return carry
+
+        lax.fori_loop(1, 2 * nt - 1, step, 0)
 
     barrier = pltpu.get_barrier_semaphore()
     for k in range(1, nt):
@@ -438,20 +488,13 @@
     weight_pass(0)
     weight_wait(0)
 
-    def project(s, carry):
-        b = other(s)
-
-        @pl.when(s > 0)
-        def _():
-            zwait(0, s, first_ref.at[blk(b)])
-
+    def project(b, s):
         out = matmul(first_ref[blk(b), :], fq[...])
         qs[blk(b), :] = (out[:, :E] + qvb_ref[0:1]).astype(bf16)
         ks[blk(b), :] = out[:, E : 2 * E].astype(bf16)
         vs[blk(b), :] = (out[:, 2 * E :] + qvb_ref[1:2]).astype(bf16)
-        return carry
-
-    lax.fori_loop(0, nt, project, 0)
+
+    gather_each(0, first_ref, project)
     for k in range(1, nt):
         zwait(1, k, segs.at[other(k)])
     weight_pass(1)
@@ -538,13 +581,7 @@
     weight_wait(2)
     small[...] = jnp.zeros_like(small)
 
-    def hidden_step(s, carry):
-        b = other(s)
-
-        @pl.when(s > 0)
-        def _():
-            zwait(3, s, second_ref.at[blk(b)])
-
+    def hidden_step(b, s):
         pre = matmul(second_ref[blk(b), :], fi[...]) + inb_ref[...]
         value, slope = gelu_pair(pre)
         act[blk(b), :] = value.astype(bf16)
@@ -557,15 +594,13 @@
         @pl.when(s > 0)
         def _():
             send[1, b] = share.astype(bf16)
-            zcopy(6, s, send.at[1, b], recv.at[1, t]).start()
+            zcopy(6, lax.rem(b - t + nt, nt), send.at[1, b], recv.at[1, t]).start()
 
         @pl.when(s == 0)
         def _():
             own[1] = share
 
-        return carry
-
-    lax.fori_loop(0, nt, hidden_step, 0)
+    gather_each(3, second_ref, hidden_step)
     for k in range(1, nt):
         sent.append(zcopy(6, k, send.at[1, other(k)], recv.at[1, t]))
 
@@ -645,17 +680,10 @@
     grad_pass(2)
     grad_pass(3)
 
-    def context_step(s, carry):
-        b = other(s)
-
-        @pl.when(s > 0)
-        def _():
-            zwait(4, s, mid_full.at[blk(b)])
-
+    def context_step(b, s):
         cg[blk(b), :] = matmul(mid_full[blk(b), :], fo[...]).astype(bf16)
-        return carry
-
-    lax.fori_loop(0, nt, context_step, 0)
+
+    gather_each(4, mid_full, context_step)
 
     for h in range(heads):
         cols = slice(h * HEAD, (h + 1) * HEAD)
@@ -744,6 +772,8 @@
     ginb_ref[...] = total[8:9, : inb_ref.shape[1]]
     ggain_ref[...] = total[0:2]
     gbias_ref[...] = total[2:6]
+    for kind, ref in ((0, first_ref), (3, second_ref), (4, mid_full)):
+        gather_drain(kind, ref)
     for copy in sent:
         copy.wait_send()
 
@@ -791,7 +821,7 @@
         + [vm((nc, rows, n), bf16) for n in widths] * 3
         + [vm((16, D), f32), vm((nt, 8, D), f32), vm((2, 16, D), f32), vm((nc, 16, D), f32)]
         + [vm((rows, n), f32) for n in (3 * E, E, F)]
-        + [pltpu.SemaphoreType.DMA((10, nt))] * 2
+        + [pltpu.SemaphoreType.DMA((10, 2 * nt))] * 2
         + [pltpu.SemaphoreType.DMA((4, 5, nc))] * 2
     )
     spec = pl.BlockSpec(memory_space=pltpu.VMEM)

time: 175 us -> 166 us (0.949)
  Pallas kernels: 160 us -> 150 us
    pallas_call x1, Pallas kernels: 160 us -> 150 us  [kernel_shards(): pl.pallas_call(functools.partial(layer_kernel, nt, nd), out_shape=[jax.Sh...]
where the time goes in v4:
time: 166 us; the launch traced here: 165 us
  Pallas kernels  150 us (90%)
  local copies, waits for them, and re-layouts  12.2 us (7%)
  other arithmetic  2.07 us (1%)
    pallas_call x1, Pallas kernels, kernel_shards(): pl.pallas_call(functools.partial(layer_kernel, nt, nd), out_shape=[jax.Sh...  150 us
    unnamed x30, local copies, waits for them, and re-layouts  10.2 us

profile of v4, /device:TPU:0, one launch (start us, length us, event | category | flops | bytes accessed | tf_op | source)
XLA Modules:
  0.0 165.2 jit_solution(9735293416192934138)
XLA Ops:
  0.6 0.0 copy-start.7
  0.7 0.7 copy-done.7
  1.3 0.0 copy-start.9
  1.3 0.6 broadcast_in_dim.18.inb_ref
  1.9 0.1 copy-done.9
  2.0 0.6 broadcast_in_dim.17.seg_ref
  2.6 1.5 copy.21
  4.1 0.9 slice_bitcast_fusion.2
  5.0 0.7 pad_maximum_fusion.wq_ref
  5.7 150.3 %layer.1 = (bf16[128,768]{1,0:T(8,128)(2,1)}, f32[128,768]{1,0:T(8,128)}, f32[3,96,192]{2,1,0:T(8,128)}, f32[192,96]{1,0:T(8,128)}, f32[96,768]{1,0:T(8,128)}, /...) custom-call(bf16[128,768]{1,0:T(8,128)(2,1)} %bitcast.17, ...), custom_call_target="tpu_custom_call" | custom-call | tf_op jit(solution)/shard_map/layer/pallas_call | solution.py:828
  156.0 0.0 copy-start
  156.0 1.3 reduce
  157.3 1.6 copy.31
  158.9 0.0 copy-done
  158.9 0.0 copy-start.3
  158.9 0.7 copy.32
  159.7 0.4 copy-done.3
  160.0 0.0 copy-start.4
  160.1 0.0 copy-start.2
  160.1 0.7 copy.33
  160.8 0.2 copy-done.4
  161.0 0.6 copy.34
  161.7 0.0 copy-done.2
  161.7 0.0 copy-start.1
  161.7 0.7 copy.35
  162.4 0.4 copy-done.1
  162.7 0.0 copy-start.8
  162.7 0.0 copy-start.6
  162.7 0.7 copy.36
  163.4 0.0 copy-done.8
  163.4 0.0 copy-start.5
  163.4 0.6 copy.37
  164.0 0.0 copy-done.6
  164.0 0.6 copy.38
  164.6 0.0 copy-done.5
  164.6 0.6 copy.39
Async XLA Ops:
  0.6 0.7 copy-start.7
  1.3 0.7 copy-start.9
  156.0 3.0 %copy-start = (f32[128,768]{1,0:T(8,128)S(1)}, f32[128,768]{1,0:T(8,128)}, u32[]{:S(2)}) copy-start(f32[128,768]{1,0:T(8,128)} %get-tuple-element.21) | copy-start | bytes 1179652
  158.9 1.1 copy-start.3
  160.0 1.0 copy-start.4
  160.1 1.6 copy-start.2
  161.7 1.1 copy-start.1
  162.7 0.7 copy-start.8
  162.7 1.3 copy-start.6
  163.4 1.2 copy-start.5
